TPU v7x, 256 devices: a whole 4x4x8 slice. The times are simulated.
256 devices in a mesh: wide: 32 (over y_hi, z, core), narrow: 8 (over x, y_lo).
Axes of the slice: x: 4, y: 4 (y_hi: 2, y_lo: 2; y = y_hi * 2 + y_lo), z: 8, core: 2. Of those that a mesh axis runs over, the one named last changes fastest.
Arguments:
- matrix: float32 [16384, 16384], P('narrow', 'wide'), may hold values from -64 to 64
Outputs:
- rotated: float32 [16384, 16384], P('narrow', 'wide')
All inputs are finite; a program needn't handle non-finite values.
Results may differ from a plain program's by a relative error of at most 0.0003.
Values sent between devices are 32-bit elements; how exact they have to be, the bound alone decides.
No kernel may reach another device: no remote copies, remote signals or barrier semaphores. Data moves between devices by JAX's collectives and lax.ppermute only.
A program may use at most 64 MiB of HBM per device.

v0:
```python
import jax
import jax.numpy as jnp
from jax import lax
from jax.sharding import PartitionSpec as P

STEPS = 2


def from_behind(value, axis, steps):
    count = lax.axis_size(axis)
    pairs = [(source, (source + steps) % count) for source in range(count)]
    return lax.ppermute(value, axis, pairs)


def product(left, right):
    return jnp.dot(left, right, precision=lax.Precision.HIGHEST)


def spd_solve(factor_low, right_side):
    first_pass = lax.linalg.triangular_solve(factor_low, right_side, left_side=True, lower=True)
    return lax.linalg.triangular_solve(
        factor_low, first_pass, left_side=True, lower=True, transpose_a=True
    )


def turn_pair(upper_block, lower_block, cross_gram, upper_norms, lower_norms):
    damped = cross_gram / (upper_norms[:, None] + lower_norms[None, :])
    block_width = damped.shape[0]
    identity = jnp.eye(block_width, dtype=damped.dtype)
    left_square = product(damped, damped.T)
    left_factor = jnp.linalg.cholesky(identity + left_square)
    solved = spd_solve(left_factor, jnp.concatenate([identity, damped], axis=1))
    inverse = solved[:, :block_width]
    inverse_damped = solved[:, block_width:]
    keep_upper = 2.0 * inverse - identity
    into_lower = 2.0 * inverse_damped
    into_upper = -2.0 * inverse_damped.T
    keep_lower = identity - 2.0 * product(damped.T, inverse_damped)
    new_upper = product(upper_block, keep_upper) + product(lower_block, into_upper)
    new_lower = product(upper_block, into_lower) + product(lower_block, keep_lower)
    return (new_upper, new_lower)


def gram_terms(upper_block, pieces):
    block_width = upper_block.shape[1]
    whole_pair = jnp.concatenate((upper_block,) + pieces, axis=1)
    summed = lax.psum(product(whole_pair.T, whole_pair), "narrow")
    diagonal = jnp.diagonal(summed)
    return (summed[:block_width, block_width:], diagonal[:block_width], diagonal[block_width:])


def move_lower(lower_block):
    return (from_behind(lower_block, "wide", 1),)


def shards(matrix):
    block_width = matrix.shape[1] // 2
    upper_block = matrix[:, :block_width]
    pieces = (matrix[:, block_width:],)
    for step_index in range(STEPS):
        cross_gram, upper_norms, lower_norms = gram_terms(upper_block, pieces)
        lower_block = pieces[0]
        upper_block, lower_block = turn_pair(
            upper_block, lower_block, cross_gram, upper_norms, lower_norms
        )
        pieces = move_lower(lower_block)
    return jnp.concatenate((upper_block,) + pieces, axis=1)


def solution(mesh):
    in_specs = (P("narrow", "wide"),)
    out_specs = P("narrow", "wide")
    return jax.shard_map(shards, mesh=mesh, in_specs=in_specs, out_specs=out_specs, check_vma=False)
```

profile of v0, /device:TPU:16, one launch (start us, length us, event | category | flops | bytes accessed | tf_op | source)
XLA Modules:
  0.0 424.8 jit_solution(5533521235223102054)
XLA Ops:
  6.5 11.2 %fusion.69 = f32[512,512]{0,1:T(8,128)} fusion(f32[2048,512]{1,0:T(8,128)} %param.6), kind=kOutput, calls=%fused_computation.131 | convolution fusion | flops 6442450944 | bytes 5242880 | tf_op jit(solution)/shard_map/dot_general | solution.py:16
  18.1 85.3 %all-reduce.4.cloned.1.call-done = f32[512,512]{0,1:T(8,128)} async-done(((f32[512,512]{0,1:T(8,128)}), f32[512,512]{0,1:T(8,128)}) %all-reduce.4.cloned.1.call-update) | async-done | bytes 1048592 | tf_op jit(solution)/shard_map/psum | solution.py:47
  103.4 8.4 %gather_fusion = f32[512]{0:T(512)S(1)} fusion(f32[512,512]{0,1:T(8,128)} %all-reduce.4.cloned.1.call-done, s32[512]{0:T(512)S(1)} %bitcast.100), kind=kCustom, calls=%fused_computation | custom fusion | bytes 8192 | tf_op jit(solution)/shard_map/jit(diagonal)/cond/branch_0_fun/gather | solution.py:48
  113.7 11.7 %cholesky.130 = f32[128,128]{1,0:T(8,128)S(1)} custom-call(f32[128,128]{1,0:T(8,128)S(1)} %cholesky.194), custom_call_target="Cholesky" | custom-call | tf_op jit(solution)/shard_map/jit(cholesky)/cholesky | solution.py:31
  125.4 9.8 %custom-call.21 = f32[1,128,128]{1,2,0:T(8,128)S(1)} custom-call(f32[1,128,128]{2,1,0:T(8,128)S(1)} %get-tuple-element.67), custom_call_target="InvertDiagBlocksLowerTriangular" | custom-call | tf_op jit(solution)/shard_map/jit(cholesky)/cholesky | solution.py:31
  135.8 11.7 %cholesky.147 = f32[128,128]{1,0:T(8,128)S(1)} custom-call(f32[128,128]{1,0:T(8,128)S(1)} %convolution_subtract_fusion.5), custom_call_target="Cholesky" | custom-call | tf_op jit(solution)/shard_map/jit(cholesky)/cholesky | solution.py:31
  149.5 3.8 while.8
  153.3 20.2 %custom-call.23 = f32[2,128,128]{1,2,0:T(8,128)S(1)} custom-call(f32[2,128,128]{2,1,0:T(8,128)S(1)} %get-tuple-element.37), custom_call_target="InvertDiagBlocksLowerTriangular" | custom-call | tf_op jit(solution)/shard_map/triangular_solve/custom-call.4 | solution.py:21
  176.9 3.7 fusion.7
  180.6 2.1 fusion.4
  184.9 3.6 convolution_add_fusion.3
  188.6 23.5 %collective-permute-done = f32[2048,256]{0,1:T(8,128)S(1)} collective-permute-done((f32[2048,256]{0,1:T(8,128)S(1)}, f32[2048,256]{0,1:T(8,128)S(1)}, u32[]{:S(2)}, u32[]{:S(2)}) %collective-permute-start) | collective-permute-done | bytes 2097184 | tf_op jit(solution)/shard_map/ppermute | solution.py:12
  213.4 8.2 %fusion = f32[512,512]{0,1:T(8,128)} fusion(f32[2048,256]{0,1:T(8,128)S(1)} %collective-permute-done, f32[2048,256]{0,1:T(8,128)S(1)} %bitcast.102), kind=kOutput, calls=%fused_computation.6 | convolution fusion | flops 6443499520 | bytes 5242880 | tf_op jit(solution)/shard_map/dot_general | solution.py:16
  221.6 80.6 %all-reduce.6.cloned.1.call-done = f32[512,512]{0,1:T(8,128)} async-done(((f32[512,512]{0,1:T(8,128)}), f32[512,512]{0,1:T(8,128)}) %all-reduce.6.cloned.1.call-update) | async-done | bytes 1048592 | tf_op jit(solution)/shard_map/psum | solution.py:47
  302.2 8.4 %gather_fusion.1 = f32[512]{0:T(512)S(1)} fusion(f32[512,512]{0,1:T(8,128)} %all-reduce.6.cloned.1.call-done, s32[512]{0:T(512)S(1)} %bitcast.101), kind=kCustom, calls=%fused_computation.1 | custom fusion | bytes 8192 | tf_op jit(solution)/shard_map/jit(diagonal)/cond/branch_0_fun/gather | solution.py:48
  312.5 11.7 %cholesky.164 = f32[128,128]{1,0:T(8,128)S(1)} custom-call(f32[128,128]{1,0:T(8,128)S(1)} %cholesky.197), custom_call_target="Cholesky" | custom-call | tf_op jit(solution)/shard_map/jit(cholesky)/cholesky | solution.py:31
  325.0 9.8 %custom-call.24 = f32[1,128,128]{1,2,0:T(8,128)S(1)} custom-call(f32[1,128,128]{2,1,0:T(8,128)S(1)} %get-tuple-element.63), custom_call_target="InvertDiagBlocksLowerTriangular" | custom-call | tf_op jit(solution)/shard_map/jit(cholesky)/cholesky | solution.py:31
  335.3 11.7 %cholesky.181 = f32[128,128]{1,0:T(8,128)S(1)} custom-call(f32[128,128]{1,0:T(8,128)S(1)} %convolution_subtract_fusion.4), custom_call_target="Cholesky" | custom-call | tf_op jit(solution)/shard_map/jit(cholesky)/cholesky | solution.py:31
  349.0 4.1 while.9
  353.1 20.1 %custom-call.26 = f32[2,128,128]{1,2,0:T(8,128)S(1)} custom-call(f32[2,128,128]{2,1,0:T(8,128)S(1)} %get-tuple-element.39), custom_call_target="InvertDiagBlocksLowerTriangular" | custom-call | tf_op jit(solution)/shard_map/triangular_solve/custom-call.4 | solution.py:21
  383.0 2.1 convolution_add_fusion.1
  385.1 24.9 %collective-permute-done.1 = f32[2048,256]{0,1:T(8,128)S(1)} collective-permute-done((f32[2048,256]{0,1:T(8,128)S(1)}, f32[2048,256]{0,1:T(8,128)S(1)}, u32[]{:S(2)}, u32[]{:S(2)}) %collective-permute-start.1) | collective-permute-done | bytes 2097184 | tf_op jit(solution)/shard_map/ppermute | solution.py:12
  410.0 2.4 pad_maximum_fusion
  412.4 5.3 %copy.27 = f32[2048,512]{1,0:T(8,128)} copy(f32[2048,512]{0,1:T(8,128)} %pad_maximum_fusion) | data formatting | bytes 8388608 | tf_op jit(solution)/shard_map/concatenate | solution.py:67
  (77 shorter events, 31.8 us)
Async XLA Ops:
  6.5 96.8 %all-reduce.4.cloned.1.call-start = ((), (), s32[]{:S(2)}) async-start(), calls=%async_computation | async-start | bytes 2097152 | tf_op jit(solution)/shard_map/psum | solution.py:47
  17.7 284.5 %all-reduce.6.cloned.1.call-start = ((), (), s32[]{:S(2)}) async-start(), calls=%async_computation.1 | async-start | bytes 2097152 | tf_op jit(solution)/shard_map/psum | solution.py:47
  176.9 3.7 copy-start
  182.7 29.3 %collective-permute-start = (f32[2048,256]{0,1:T(8,128)S(1)}, f32[2048,256]{0,1:T(8,128)S(1)}, u32[]{:S(2)}, u32[]{:S(2)}) collective-permute-start(f32[2048,256]{0,1:T(8,128)S(1)} %fusion.4), channel_id=1, source_target_pairs={{0,8},{8,16},{16,24},{24,32},{32,40},{40,48},{48,56},{56,64},{64,7... | collective-permute-start | bytes 6291464 | tf_op jit(solution)/shard_map/ppermute | solution.py:12
  212.0 1.3 copy-start.1
  376.5 2.1 copy-start.2
  380.7 29.3 %collective-permute-start.1 = (f32[2048,256]{0,1:T(8,128)S(1)}, f32[2048,256]{0,1:T(8,128)S(1)}, u32[]{:S(2)}, u32[]{:S(2)}) collective-permute-start(f32[2048,256]{0,1:T(8,128)S(1)} %convolution_add_fusion), channel_id=1, source_target_pairs={{0,8},{8,16},{16,24},{24,32},{32,40},{40,48},{48,56},{56,64},{64,7... | collective-permute-start | bytes 6291464 | tf_op jit(solution)/shard_map/ppermute | solution.py:12
Sparse Core Ops, SparseCore 0:
  17.8 85.4 all-reduce.3
  221.7 80.4 all-reduce.5
where the time goes:
time: 429 us; the launch traced here: 425 us
  waiting for transfers between devices  214 us (50%)
  other arithmetic  114 us (27%)
  matrix products  47.5 us (11%)
  local copies, waits for them, and re-layouts  32 us (7%)
  between operations  16.5 us (4%)
    psum x2, waiting for transfers between devices, gram_terms(): summed = lax.psum(product(whole_pair.T, whole_pair), 'narrow')  166 us
    another operation x13, other arithmetic, turn_pair(): left_factor = jnp.linalg.cholesky(identity + left_square)  68.6 us
    ppermute x2, waiting for transfers between devices, from_behind(): return lax.ppermute(value, axis, pairs)  48.4 us
    dot_general x14, matrix products, product(): return jnp.dot(left, right, precision=lax.Precision.HIGHEST)  41 us
    another operation x5, other arithmetic, spd_solve(): lax.linalg.triangular_solve(factor_low, first_pass, left_side=True, lower...  40.3 us
    gather x2, local copies, waits for them, and re-layouts, gram_terms(): diagonal = jnp.diagonal(summed)  16.8 us
  transfers between devices with their start and end apart: 4, of which 4 were waited for; matrix products, arithmetic and copies ran while one was open for 2% of the time, Pallas kernels for 0%

commit v1 on v0

v1 whole, which is shorter than its diff:
```python
import functools

import jax
import jax.numpy as jnp
from jax import lax
from jax.experimental import pallas as pl
from jax.experimental.pallas import tpu as pltpu
from jax.sharding import PartitionSpec as P

PIECES = 4
MEMBERS = 8
TAIL = 8
ROUNDS = (1, 2, 6)
F32 = jnp.float32
BF16 = jnp.bfloat16
PLAIN = (((1,), (0,)), ((), ()))
ROWS_FIRST = (((0,), (0,)), ((), ()))
COLS_LAST = (((1,), (1,)), ((), ()))
VMEM = pl.BlockSpec(memory_space=pltpu.VMEM)
MIB = 1 << 20


def halves(value):
    high = value.astype(BF16)
    return high, (value - high.astype(F32)).astype(BF16)


def dot(left, right, dims=PLAIN):
    return lax.dot_general(left, right, dims, preferred_element_type=F32)


def exact(left, right, dims=PLAIN):
    return lax.dot_general(
        left, right, dims, precision=lax.Precision.HIGHEST, preferred_element_type=F32
    )


def part_of(upper, lower):
    upper_high, upper_low = halves(upper)
    lower_high, lower_low = halves(lower)
    cross = dot(upper_high, lower_high, ROWS_FIRST)
    cross += dot(upper_high, lower_low, ROWS_FIRST)
    cross += dot(upper_low, lower_high, ROWS_FIRST)
    width = upper.shape[1]
    row = lax.broadcasted_iota(jnp.int32, (TAIL, width), 0)
    norms = jnp.where(row == 0, jnp.sum(upper * upper, axis=0, keepdims=True), 0.0)
    norms = jnp.where(row == 1, jnp.sum(lower * lower, axis=0, keepdims=True), norms)
    return cross, norms


def first_gram_body(upper_ref, lower_ref, out_ref):
    width = upper_ref.shape[1]
    cross, norms = part_of(upper_ref[...], lower_ref[...])

    @pl.when(pl.program_id(0) == 0)
    def _():
        out_ref[:width] = cross
        out_ref[width:] = norms

    @pl.when(pl.program_id(0) > 0)
    def _():
        out_ref[:width] += cross
        out_ref[width:] += norms


def first_gram(matrix, tile=1024):
    rows, width = matrix.shape[0], matrix.shape[1] // 2
    return pl.pallas_call(
        first_gram_body,
        grid=(rows // tile,),
        in_specs=[
            pl.BlockSpec((tile, width), lambda i: (i, 0)),
            pl.BlockSpec((tile, width), lambda i: (i, 1)),
        ],
        out_specs=pl.BlockSpec((width + TAIL, width), lambda i: (0, 0)),
        out_shape=jax.ShapeDtypeStruct((width + TAIL, width), F32),
        compiler_params=pltpu.CompilerParams(vmem_limit_bytes=8 * MIB),
        name="first_gram",
    )(matrix, matrix)


def gram_body(tile, count, upper_ref, *refs):
    lower_refs, out_ref = refs[:count], refs[-1]
    width = upper_ref.shape[1]
    start, total = 0, None
    for lower_ref in lower_refs:
        for at in range(0, lower_ref.shape[0], tile):
            part = part_of(upper_ref[pl.ds(start, tile), :], lower_ref[pl.ds(at, tile), :])
            total = part if total is None else tuple(a + b for a, b in zip(total, part))
            start += tile
    out_ref[:width], out_ref[width:] = total


def gram(upper, lowers, after=(), tile=512):
    width = upper.shape[1]
    return pl.pallas_call(
        functools.partial(gram_body, tile, len(lowers)),
        in_specs=[VMEM] * (1 + len(lowers)) + [pl.BlockSpec(memory_space=pl.ANY)] * len(after),
        out_specs=VMEM,
        out_shape=jax.ShapeDtypeStruct((width + TAIL, width), F32),
        compiler_params=pltpu.CompilerParams(vmem_limit_bytes=8 * MIB),
        name="gram",
    )(upper, *lowers, *after)


def solve_body(left_ref, right_ref, high_ref, low_ref, inverse_ref):
    width = left_ref.shape[1]
    cross = left_ref[:width] + right_ref[:width]
    norms = left_ref[width:] + right_ref[width:]
    row = lax.broadcasted_iota(jnp.int32, (width, width), 0)
    column = lax.broadcasted_iota(jnp.int32, (width, width), 1)
    identity = jnp.where(row == column, 1.0, 0.0).astype(F32)
    upper_norms = jnp.sum(jnp.where(row == column, norms[0:1], 0.0), axis=1, keepdims=True)
    damped = cross / (upper_norms + norms[1:2])
    square = exact(damped, damped, COLS_LAST)
    bound = jnp.max(jnp.sum(jnp.abs(square), axis=0))
    scale = 2.0 / (2.0 + bound)
    whole = identity + square
    inverse_ref[...] = scale * (2.0 * identity - scale * whole)

    def more(state):
        count, off = state
        return jnp.logical_and(count < 40, off > 1e-3)

    def refine(state):
        count, _ = state
        inverse = inverse_ref[...]
        rest = identity - exact(whole, inverse)
        inverse_ref[...] = inverse + exact(inverse, rest)
        return count + 1, jnp.max(jnp.sum(jnp.abs(rest), axis=0))

    lax.while_loop(more, refine, (jnp.int32(0), jnp.float32(1.0)))
    inverse = inverse_ref[...]
    into_lower = 2.0 * exact(inverse, damped)
    into_upper = -into_lower.T
    keep_lower = identity + exact(into_upper, damped)
    for place, block in (
        ((0, 0), 2.0 * inverse - identity),
        ((0, 1), into_lower),
        ((1, 0), into_upper),
        ((1, 1), keep_lower),
    ):
        high, low = halves(block)
        at = (pl.ds(place[0] * width, width), pl.ds(place[1] * width, width))
        high_ref[at] = high
        low_ref[at] = low


def solve(left, right):
    width = left.shape[1]
    out = jax.ShapeDtypeStruct((2 * width, 2 * width), BF16)
    return pl.pallas_call(
        solve_body,
        in_specs=[VMEM] * 2,
        out_specs=(VMEM, VMEM),
        out_shape=(out, out),
        scratch_shapes=[pltpu.VMEM((width, width), F32)],
        compiler_params=pltpu.CompilerParams(vmem_limit_bytes=8 * MIB),
        name="solve",
    )(left, right)


def turn_rows(block_refs, starts, high_ref, low_ref, side, at, tile):
    width = 256
    columns = pl.ds(side * width, width)
    total, depth = None, 0
    for ref, first in zip(block_refs, starts):
        high, low = halves(ref[pl.ds(first + at, tile), :])
        rows = pl.ds(depth, high.shape[1])
        turn_high, turn_low = high_ref[rows, columns], low_ref[rows, columns]
        part = dot(high, turn_high) + dot(low, turn_high) + dot(high, turn_low)
        total = part if total is None else total + part
        depth += high.shape[1]
    return total


def turn_body(side, starts, tile, *refs):
    *block_refs, high_ref, low_ref, out_ref = refs
    for at in range(0, out_ref.shape[0], tile):
        total = turn_rows(block_refs, starts, high_ref, low_ref, side, at, tile)
        out_ref[pl.ds(at, tile), :] = total


def turn(blocks, turns, side, starts, rows, tile=512):
    return pl.pallas_call(
        functools.partial(turn_body, side, starts, tile),
        in_specs=[VMEM] * (len(blocks) + 2),
        out_specs=VMEM,
        out_shape=jax.ShapeDtypeStruct((rows, 256), F32),
        compiler_params=pltpu.CompilerParams(vmem_limit_bytes=8 * MIB),
        name="turn_lower" if side else "turn_upper",
    )(*blocks, *turns)


def last_body(tile, flag_ref, upper_ref, *refs):
    *others, out_ref = refs
    half = len(others) // 2
    for want, sources in ((1, others[:half]), (0, others[half:])):

        @pl.when(flag_ref[0] == want)
        def _(sources=sources):
            *lower_refs, high_ref, low_ref = sources
            at = 0
            for lower_ref in lower_refs:
                for inner in range(0, lower_ref.shape[0], tile):
                    total = turn_rows(
                        (upper_ref, lower_ref), (at - inner, 0), high_ref, low_ref, 0, inner, tile
                    )
                    out_ref[pl.ds(at, tile), :256] = total
                    at += tile


def last_upper(flag, upper, near, turns_near, far, turns_far, tile=512):
    rows, width = upper.shape
    others = [*near, *turns_near, *far, *turns_far]
    return pl.pallas_call(
        functools.partial(last_body, tile),
        in_specs=[pl.BlockSpec(memory_space=pltpu.SMEM)] + [VMEM] * (1 + len(others)),
        out_specs=VMEM,
        out_shape=jax.ShapeDtypeStruct((rows, 2 * width), F32),
        compiler_params=pltpu.CompilerParams(vmem_limit_bytes=8 * MIB),
        name="last_upper",
    )(flag, upper, *others)


def move(value, target):
    wide, narrow = lax.axis_size("wide"), lax.axis_size("narrow")
    pairs = []
    for w in range(wide):
        for n in range(narrow):
            to = target(w, n)
            if to is not None:
                pairs.append((w * narrow + n, (to[0] % wide) * narrow + to[1]))
    return lax.ppermute(value, ("wide", "narrow"), pairs)


def all_sum(value, active=None):
    for k, mask in enumerate(ROUNDS):
        other = move(
            value, lambda w, n: (w, n ^ mask if active is None or w % 2 == active else n)
        )
        if k + 1 == len(ROUNDS):
            return value, other
        value = value + other


def within(w, n):
    return w ^ 1, n


def across(w, n):
    return (w + 1 if w % 2 else w - 1), n


def to_odd(w, n):
    return None if w % 2 else (w + 1, n)


def to_even(w, n):
    return (w + 1, n) if w % 2 else None


def last_one_body(tile, upper_ref, *refs):
    *lower_refs, high_ref, low_ref, out_ref = refs
    at = 0
    for lower_ref in lower_refs:
        for inner in range(0, lower_ref.shape[0], tile):
            total = turn_rows((upper_ref, lower_ref), (at - inner, 0), high_ref, low_ref, 0, inner, tile)
            out_ref[pl.ds(at, tile), :256] = total
            at += tile


def last_one(upper, lowers, turns, tile=512):
    rows, width = upper.shape
    others = [*lowers, *turns]
    return pl.pallas_call(
        functools.partial(last_one_body, tile),
        in_specs=[VMEM] * (1 + len(others)),
        out_specs=VMEM,
        out_shape=jax.ShapeDtypeStruct((rows, 2 * width), F32),
        compiler_params=pltpu.CompilerParams(vmem_limit_bytes=8 * MIB),
        name="last_upper",
    )(upper, *others)


def onward(w, n):
    return w + 1, n


def shards(matrix):
    rows, width = matrix.shape[0], matrix.shape[1] // 2
    piece = rows // PIECES
    starts = [k * piece for k in range(PIECES)]
    turns = solve(*all_sum(first_gram(matrix)))
    lowers = [move(turn([matrix], turns, 1, (at,), piece), onward) for at in starts]
    upper = turn([matrix], turns, 0, (0,), rows)
    turns = solve(*all_sum(gram(upper, lowers)))
    last = [
        move(turn([upper, lowers[k]], turns, 1, (at, 0), piece), onward)
        for k, at in enumerate(starts)
    ]
    out = last_one(upper, lowers, turns)
    for k, at in enumerate(starts):
        out = lax.dynamic_update_slice(out, last[k], (at, width))
    return out


def solution(mesh):
    spec = P("narrow", "wide")
    return jax.shard_map(shards, mesh=mesh, in_specs=(spec,), out_specs=spec, check_vma=False)
```

time: 429 us -> 143 us (0.33)
  waiting for transfers between devices: 214 us -> 75.5 us
  other arithmetic: 114 us -> 0.14 us
  matrix products: 47.5 us -> 0 us
  Pallas kernels: 0 us -> 43.4 us
  local copies, waits for them, and re-layouts: 32 us -> 5.5 us
  starting transfers between devices: 0.85 us -> 17.6 us
  between operations: 16.5 us -> 0.15 us
    psum x2 -> x0, waiting for transfers between devices: 166 us -> none  [gram_terms(): summed = lax.psum(product(whole_pair.T, whole_pair), 'narrow')]
    another operation x18 -> x0, other arithmetic: 109 us -> none  [the longest x13 68.6 us: turn_pair(): left_factor = jnp.linalg.cholesky(identity + left_square)]
    pallas_call x0 -> x14, Pallas kernels: none -> 43.4 us  [the longest x2 30.1 us: solve(): pl.pallas_call(solve_body, in_specs=[VMEM] * 2, out_specs=(VMEM, VMEM), o...]
    dot_general x14 -> x0, matrix products: 41 us -> none  [product(): return jnp.dot(left, right, precision=lax.Precision.HIGHEST)]
    ppermute x2 -> x14, waiting for transfers between devices: 48.4 us -> 75.5 us  [move(): return lax.ppermute(value, ('wide', 'narrow'), pairs)]
    ppermute x2 -> x14, starting transfers between devices: 0.51 us -> 17.6 us  [move(): return lax.ppermute(value, ('wide', 'narrow'), pairs)]
    gather x2 -> x0, local copies, waits for them, and re-layouts: 16.8 us -> none  [gram_terms(): diagonal = jnp.diagonal(summed)]
    another operation x21 -> x0, local copies, waits for them, and re-layouts: 8.18 us -> none  [the longest x17 8.13 us: spd_solve(): lax.linalg.triangular_solve(factor_low, first_pass, left_side=True, lower...]
  transfers between devices with their start and end apart: 4 -> 14, of which waited for: 4 -> 14; matrix products, arithmetic and copies ran while one was open for 2% -> 2% of each run, Pallas kernels for 0% -> 5%
where the time goes in v1:
time: 143 us; the launch traced here: 142 us
  waiting for transfers between devices  75.5 us (53%)
  Pallas kernels  43.4 us (30%)
  starting transfers between devices  17.6 us (12%)
  local copies, waits for them, and re-layouts  5.5 us (4%)
    ppermute x14, waiting for transfers between devices, move(): return lax.ppermute(value, ('wide', 'narrow'), pairs)  75.5 us
    pallas_call x2, Pallas kernels, solve(): pl.pallas_call(solve_body, in_specs=[VMEM] * 2, out_specs=(VMEM, VMEM), o...  30.1 us
    ppermute x14, starting transfers between devices, move(): return lax.ppermute(value, ('wide', 'narrow'), pairs)  17.6 us
    pallas_call x9, Pallas kernels, turn(): pl.pallas_call(functools.partial(turn_body, side, starts, tile), in_specs...  6.43 us
    pallas_call x1, Pallas kernels, last_one(): pl.pallas_call(functools.partial(last_one_body, tile), in_specs=[VMEM] *...  3.82 us
    dynamic_update_slice x4, local copies, waits for them, and re-layouts, shards(): out = lax.dynamic_update_slice(out, last[k], (at, width))  3.31 us
  transfers between devices with their start and end apart: 14, of which 14 were waited for; matrix products, arithmetic and copies ran while one was open for 2% of the time, Pallas kernels for 5%

profile of v1, /device:TPU:16, one launch (start us, length us, event | category | flops | bytes accessed | tf_op | source)
XLA Modules:
  0.0 142.3 jit_solution(11731266400620175727)
XLA Ops:
  0.0 2.2 %copy-done = f32[2048,512]{1,0:T(8,128)S(1)} copy-done((f32[2048,512]{1,0:T(8,128)S(1)}, f32[2048,512]{1,0:T(8,128)}, u32[]{:S(2)}) %copy-start) | copy-done | bytes 4194328
  2.2 1.8 %first_gram.1 = f32[264,256]{1,0:T(8,128)S(1)} custom-call(f32[2048,512]{1,0:T(8,128)S(1)} %copy-done, f32[2048,512]{1,0:T(8,128)S(1)} %copy-done), custom_call_target="tpu_custom_call" | custom-call | tf_op jit(solution)/shard_map/first_gram/pallas_call | solution.py:68
  5.4 6.9 %collective-permute-done = f32[264,256]{1,0:T(8,128)S(1)} collective-permute-done((f32[264,256]{1,0:T(8,128)S(1)}, f32[264,256]{1,0:T(8,128)S(1)}, u32[]{:S(2)}, u32[]{:S(2)}) %collective-permute-start) | collective-permute-done | bytes 270368 | tf_op jit(solution)/shard_map/ppermute | solution.py:234
  13.9 5.9 %collective-permute-done.1 = f32[264,256]{1,0:T(8,128)S(1)} collective-permute-done((f32[264,256]{1,0:T(8,128)S(1)}, f32[264,256]{1,0:T(8,128)S(1)}, u32[]{:S(2)}, u32[]{:S(2)}) %collective-permute-start.1) | collective-permute-done | bytes 270368 | tf_op jit(solution)/shard_map/ppermute | solution.py:234
  19.9 2.8 %collective-permute-start.2 = (f32[264,256]{1,0:T(8,128)S(1)}, f32[264,256]{1,0:T(8,128)S(1)}, u32[]{:S(2)}, u32[]{:S(2)}) collective-permute-start(f32[264,256]{1,0:T(8,128)S(1)} %add.13.left_ref), channel_id=1, source_target_pairs={{0,6},{1,7},{2,4},{3,5},{4,2},{5,3},{6,0},{7,1},{8,14},{9,15},{10,... | collective-permute-start | bytes 811016 | tf_op jit(solution)/shard_map/ppermute | solution.py:234
  22.7 5.0 %collective-permute-done.2.right_ref = f32[264,256]{1,0:T(8,128)S(1)} collective-permute-done((f32[264,256]{1,0:T(8,128)S(1)}, f32[264,256]{1,0:T(8,128)S(1)}, u32[]{:S(2)}, u32[]{:S(2)}) %collective-permute-start.2) | collective-permute-done | bytes 270368 | tf_op jit(solution)/shard_map/ppermute | solution.py:234
  27.7 15.1 %solve.2 = (bf16[512,512]{1,0:T(8,128)(2,1)S(1)}, bf16[512,512]{1,0:T(8,128)(2,1)S(1)}) custom-call(f32[264,256]{1,0:T(8,128)S(1)} %add.13.left_ref, f32[264,256]{1,0:T(8,128)S(1)} %collective-permute-done.2.right_ref), custom_call_target="tpu_custom_call" | custom-call | tf_op jit(solution)/shard_map/solve/pallas_call | solution.py:152
  45.2 2.0 %collective-permute-start.4 = (f32[512,256]{1,0:T(8,128)S(1)}, f32[512,256]{1,0:T(8,128)S(1)}, u32[]{:S(2)}, u32[]{:S(2)}) collective-permute-start(f32[512,256]{1,0:T(8,128)S(1)} %turn_lower.9), channel_id=1, source_target_pairs={{0,8},{1,9},{2,10},{3,11},{4,12},{5,13},{6,14},{7,15},{8,16},{9,17... | collective-permute-start | bytes 1572872 | tf_op jit(solution)/shard_map/ppermute | solution.py:234
  47.3 2.0 %collective-permute-start.6 = (f32[512,256]{1,0:T(8,128)S(1)}, f32[512,256]{1,0:T(8,128)S(1)}, u32[]{:S(2)}, u32[]{:S(2)}) collective-permute-start(f32[512,256]{1,0:T(8,128)S(1)} %turn_lower.11), channel_id=1, source_target_pairs={{0,8},{1,9},{2,10},{3,11},{4,12},{5,13},{6,14},{7,15},{8,16},{9,17... | collective-permute-start | bytes 1572872 | tf_op jit(solution)/shard_map/ppermute | solution.py:234
  51.0 6.4 %collective-permute-done.3.refs_0_.refs_1_ = f32[512,256]{1,0:T(8,128)S(1)} collective-permute-done((f32[512,256]{1,0:T(8,128)S(1)}, f32[512,256]{1,0:T(8,128)S(1)}, u32[]{:S(2)}, u32[]{:S(2)}) %collective-permute-start.3) | collective-permute-done | bytes 524320 | tf_op jit(solution)/shard_map/ppermute | solution.py:234
  57.4 5.6 %collective-permute-done.4.refs_1_ = f32[512,256]{1,0:T(8,128)S(1)} collective-permute-done((f32[512,256]{1,0:T(8,128)S(1)}, f32[512,256]{1,0:T(8,128)S(1)}, u32[]{:S(2)}, u32[]{:S(2)}) %collective-permute-start.4) | collective-permute-done | bytes 524320 | tf_op jit(solution)/shard_map/ppermute | solution.py:234
  63.0 5.6 %collective-permute-done.5.refs_2_.refs_1_ = f32[512,256]{1,0:T(8,128)S(1)} collective-permute-done((f32[512,256]{1,0:T(8,128)S(1)}, f32[512,256]{1,0:T(8,128)S(1)}, u32[]{:S(2)}, u32[]{:S(2)}) %collective-permute-start.5) | collective-permute-done | bytes 524320 | tf_op jit(solution)/shard_map/ppermute | solution.py:234
  68.6 5.6 %collective-permute-done.6.refs_3_.refs_1_ = f32[512,256]{1,0:T(8,128)S(1)} collective-permute-done((f32[512,256]{1,0:T(8,128)S(1)}, f32[512,256]{1,0:T(8,128)S(1)}, u32[]{:S(2)}, u32[]{:S(2)}) %collective-permute-start.6) | collective-permute-done | bytes 524320 | tf_op jit(solution)/shard_map/ppermute | solution.py:234
  77.1 5.2 %collective-permute-done.7 = f32[264,256]{1,0:T(8,128)S(1)} collective-permute-done((f32[264,256]{1,0:T(8,128)S(1)}, f32[264,256]{1,0:T(8,128)S(1)}, u32[]{:S(2)}, u32[]{:S(2)}) %collective-permute-start.7) | collective-permute-done | bytes 270368 | tf_op jit(solution)/shard_map/ppermute | solution.py:234
  82.6 6.2 %collective-permute-done.8 = f32[264,256]{1,0:T(8,128)S(1)} collective-permute-done((f32[264,256]{1,0:T(8,128)S(1)}, f32[264,256]{1,0:T(8,128)S(1)}, u32[]{:S(2)}, u32[]{:S(2)}) %collective-permute-start.8) | collective-permute-done | bytes 270368 | tf_op jit(solution)/shard_map/ppermute | solution.py:234
  88.9 2.8 %collective-permute-start.9 = (f32[264,256]{1,0:T(8,128)S(1)}, f32[264,256]{1,0:T(8,128)S(1)}, u32[]{:S(2)}, u32[]{:S(2)}) collective-permute-start(f32[264,256]{1,0:T(8,128)S(1)} %add.15.left_ref), channel_id=1, source_target_pairs={{0,6},{1,7},{2,4},{3,5},{4,2},{5,3},{6,0},{7,1},{8,14},{9,15},{10,... | collective-permute-start | bytes 811016 | tf_op jit(solution)/shard_map/ppermute | solution.py:234
  91.7 4.9 %collective-permute-done.9.right_ref = f32[264,256]{1,0:T(8,128)S(1)} collective-permute-done((f32[264,256]{1,0:T(8,128)S(1)}, f32[264,256]{1,0:T(8,128)S(1)}, u32[]{:S(2)}, u32[]{:S(2)}) %collective-permute-start.9) | collective-permute-done | bytes 270368 | tf_op jit(solution)/shard_map/ppermute | solution.py:234
  96.6 15.1 %solve.3 = (bf16[512,512]{1,0:T(8,128)(2,1)S(1)}, bf16[512,512]{1,0:T(8,128)(2,1)S(1)}) custom-call(f32[264,256]{1,0:T(8,128)S(1)} %add.15.left_ref, f32[264,256]{1,0:T(8,128)S(1)} %collective-permute-done.9.right_ref), custom_call_target="tpu_custom_call" | custom-call | tf_op jit(solution)/shard_map/solve/pallas_call | solution.py:152
  114.8 2.1 %collective-permute-start.13 = (f32[512,256]{1,0:T(8,128)S(1)}, f32[512,256]{1,0:T(8,128)S(1)}, u32[]{:S(2)}, u32[]{:S(2)}) collective-permute-start(f32[512,256]{1,0:T(8,128)S(1)} %turn_lower.15), channel_id=1, source_target_pairs={{0,8},{1,9},{2,10},{3,11},{4,12},{5,13},{6,14},{7,15},{8,16},{9,17... | collective-permute-start | bytes 1572872 | tf_op jit(solution)/shard_map/ppermute | solution.py:234
  116.9 3.8 %last_upper.1 = f32[2048,512]{1,0:T(8,128)} custom-call(f32[2048,256]{1,0:T(8,128)S(1)} %turn_upper.1.upper_ref.refs_0_, f32[512,256]{1,0:T(8,128)S(1)} %collective-permute-done.3.refs_0_.refs_1_, f32[512,256]{1,0:T(8,128)S(1)} %collective-permute-done.4.refs_1_, f32[512,256]{1,0:T(8,128)S(1)} %collective-permute-done.5.refs_2_.refs_1_, ...), custom_call_target="tpu_custom_call" | custom-call | tf_op jit(solution)/shard_map/last_upper/pallas_call | solution.py:276
  120.7 3.9 %collective-permute-done.10 = f32[512,256]{1,0:T(8,128)S(1)} collective-permute-done((f32[512,256]{1,0:T(8,128)S(1)}, f32[512,256]{1,0:T(8,128)S(1)}, u32[]{:S(2)}, u32[]{:S(2)}) %collective-permute-start.10) | collective-permute-done | bytes 524320 | tf_op jit(solution)/shard_map/ppermute | solution.py:234
  125.4 4.8 %collective-permute-done.11 = f32[512,256]{1,0:T(8,128)S(1)} collective-permute-done((f32[512,256]{1,0:T(8,128)S(1)}, f32[512,256]{1,0:T(8,128)S(1)}, u32[]{:S(2)}, u32[]{:S(2)}) %collective-permute-start.11) | collective-permute-done | bytes 524320 | tf_op jit(solution)/shard_map/ppermute | solution.py:234
  131.0 4.8 %collective-permute-done.12 = f32[512,256]{1,0:T(8,128)S(1)} collective-permute-done((f32[512,256]{1,0:T(8,128)S(1)}, f32[512,256]{1,0:T(8,128)S(1)}, u32[]{:S(2)}, u32[]{:S(2)}) %collective-permute-start.12) | collective-permute-done | bytes 524320 | tf_op jit(solution)/shard_map/ppermute | solution.py:234
  136.6 4.8 %collective-permute-done.13 = f32[512,256]{1,0:T(8,128)S(1)} collective-permute-done((f32[512,256]{1,0:T(8,128)S(1)}, f32[512,256]{1,0:T(8,128)S(1)}, u32[]{:S(2)}, u32[]{:S(2)}) %collective-permute-start.13) | collective-permute-done | bytes 524320 | tf_op jit(solution)/shard_map/ppermute | solution.py:234
  (30 shorter events, 16.9 us)
Async XLA Ops:
  0.0 2.2 %copy-start = (f32[2048,512]{1,0:T(8,128)S(1)}, f32[2048,512]{1,0:T(8,128)}, u32[]{:S(2)}) copy-start(f32[2048,512]{1,0:T(8,128)} %refs_0_.9) | copy-start | bytes 12582916
  2.2 40.6 %copy-start.1 = (f32[2048,512]{1,0:T(8,128)S(1)}, f32[2048,512]{1,0:T(8,128)}, u32[]{:S(2)}) copy-start(f32[2048,512]{1,0:T(8,128)} %refs_0_.9) | copy-start | bytes 12582916
  4.0 8.3 %collective-permute-start = (f32[264,256]{1,0:T(8,128)S(1)}, f32[264,256]{1,0:T(8,128)S(1)}, u32[]{:S(2)}, u32[]{:S(2)}) collective-permute-start(f32[264,256]{1,0:T(8,128)S(1)} %first_gram.1), channel_id=1, source_target_pairs={{0,1},{1,0},{2,3},{3,2},{4,5},{5,4},{6,7},{7,6},{8,9},{9,8},{10,11... | collective-permute-start | bytes 811016 | tf_op jit(solution)/shard_map/ppermute | solution.py:234
  12.4 7.5 %collective-permute-start.1 = (f32[264,256]{1,0:T(8,128)S(1)}, f32[264,256]{1,0:T(8,128)S(1)}, u32[]{:S(2)}, u32[]{:S(2)}) collective-permute-start(f32[264,256]{1,0:T(8,128)S(1)} %add.12), channel_id=1, source_target_pairs={{0,2},{1,3},{2,0},{3,1},{4,6},{5,7},{6,4},{7,5},{8,10},{9,11},{10,... | collective-permute-start | bytes 811016 | tf_op jit(solution)/shard_map/ppermute | solution.py:234
  19.9 7.8 %collective-permute-start.2 = (f32[264,256]{1,0:T(8,128)S(1)}, f32[264,256]{1,0:T(8,128)S(1)}, u32[]{:S(2)}, u32[]{:S(2)}) collective-permute-start(f32[264,256]{1,0:T(8,128)S(1)} %add.13.left_ref), channel_id=1, source_target_pairs={{0,6},{1,7},{2,4},{3,5},{4,2},{5,3},{6,0},{7,1},{8,14},{9,15},{10,... | collective-permute-start | bytes 811016 | tf_op jit(solution)/shard_map/ppermute | solution.py:234
  45.1 12.3 %collective-permute-start.3 = (f32[512,256]{1,0:T(8,128)S(1)}, f32[512,256]{1,0:T(8,128)S(1)}, u32[]{:S(2)}, u32[]{:S(2)}) collective-permute-start(f32[512,256]{1,0:T(8,128)S(1)} %turn_lower.8), channel_id=1, source_target_pairs={{0,8},{1,9},{2,10},{3,11},{4,12},{5,13},{6,14},{7,15},{8,16},{9,17... | collective-permute-start | bytes 1572872 | tf_op jit(solution)/shard_map/ppermute | solution.py:234
  45.2 17.8 %collective-permute-start.4 = (f32[512,256]{1,0:T(8,128)S(1)}, f32[512,256]{1,0:T(8,128)S(1)}, u32[]{:S(2)}, u32[]{:S(2)}) collective-permute-start(f32[512,256]{1,0:T(8,128)S(1)} %turn_lower.9), channel_id=1, source_target_pairs={{0,8},{1,9},{2,10},{3,11},{4,12},{5,13},{6,14},{7,15},{8,16},{9,17... | collective-permute-start | bytes 1572872 | tf_op jit(solution)/shard_map/ppermute | solution.py:234
  47.2 21.5 %collective-permute-start.5 = (f32[512,256]{1,0:T(8,128)S(1)}, f32[512,256]{1,0:T(8,128)S(1)}, u32[]{:S(2)}, u32[]{:S(2)}) collective-permute-start(f32[512,256]{1,0:T(8,128)S(1)} %turn_lower.10), channel_id=1, source_target_pairs={{0,8},{1,9},{2,10},{3,11},{4,12},{5,13},{6,14},{7,15},{8,16},{9,17... | collective-permute-start | bytes 1572872 | tf_op jit(solution)/shard_map/ppermute | solution.py:234
  47.3 27.0 %collective-permute-start.6 = (f32[512,256]{1,0:T(8,128)S(1)}, f32[512,256]{1,0:T(8,128)S(1)}, u32[]{:S(2)}, u32[]{:S(2)}) collective-permute-start(f32[512,256]{1,0:T(8,128)S(1)} %turn_lower.11), channel_id=1, source_target_pairs={{0,8},{1,9},{2,10},{3,11},{4,12},{5,13},{6,14},{7,15},{8,16},{9,17... | collective-permute-start | bytes 1572872 | tf_op jit(solution)/shard_map/ppermute | solution.py:234
  75.5 6.7 %collective-permute-start.7 = (f32[264,256]{1,0:T(8,128)S(1)}, f32[264,256]{1,0:T(8,128)S(1)}, u32[]{:S(2)}, u32[]{:S(2)}) collective-permute-start(f32[264,256]{1,0:T(8,128)S(1)} %gram.1), channel_id=1, source_target_pairs={{0,1},{1,0},{2,3},{3,2},{4,5},{5,4},{6,7},{7,6},{8,9},{9,8},{10,11... | collective-permute-start | bytes 811016 | tf_op jit(solution)/shard_map/ppermute | solution.py:234
  82.3 6.5 %collective-permute-start.8 = (f32[264,256]{1,0:T(8,128)S(1)}, f32[264,256]{1,0:T(8,128)S(1)}, u32[]{:S(2)}, u32[]{:S(2)}) collective-permute-start(f32[264,256]{1,0:T(8,128)S(1)} %add.14), channel_id=1, source_target_pairs={{0,2},{1,3},{2,0},{3,1},{4,6},{5,7},{6,4},{7,5},{8,10},{9,11},{10,... | collective-permute-start | bytes 811016 | tf_op jit(solution)/shard_map/ppermute | solution.py:234
  88.9 7.8 %collective-permute-start.9 = (f32[264,256]{1,0:T(8,128)S(1)}, f32[264,256]{1,0:T(8,128)S(1)}, u32[]{:S(2)}, u32[]{:S(2)}) collective-permute-start(f32[264,256]{1,0:T(8,128)S(1)} %add.15.left_ref), channel_id=1, source_target_pairs={{0,6},{1,7},{2,4},{3,5},{4,2},{5,3},{6,0},{7,1},{8,14},{9,15},{10,... | collective-permute-start | bytes 811016 | tf_op jit(solution)/shard_map/ppermute | solution.py:234
  112.3 12.3 %collective-permute-start.10 = (f32[512,256]{1,0:T(8,128)S(1)}, f32[512,256]{1,0:T(8,128)S(1)}, u32[]{:S(2)}, u32[]{:S(2)}) collective-permute-start(f32[512,256]{1,0:T(8,128)S(1)} %turn_lower.12), channel_id=1, source_target_pairs={{0,8},{1,9},{2,10},{3,11},{4,12},{5,13},{6,14},{7,15},{8,16},{9,17... | collective-permute-start | bytes 1572872 | tf_op jit(solution)/shard_map/ppermute | solution.py:234
  113.0 17.2 %collective-permute-start.11 = (f32[512,256]{1,0:T(8,128)S(1)}, f32[512,256]{1,0:T(8,128)S(1)}, u32[]{:S(2)}, u32[]{:S(2)}) collective-permute-start(f32[512,256]{1,0:T(8,128)S(1)} %turn_lower.13), channel_id=1, source_target_pairs={{0,8},{1,9},{2,10},{3,11},{4,12},{5,13},{6,14},{7,15},{8,16},{9,17... | collective-permute-start | bytes 1572872 | tf_op jit(solution)/shard_map/ppermute | solution.py:234
  114.1 21.7 %collective-permute-start.12 = (f32[512,256]{1,0:T(8,128)S(1)}, f32[512,256]{1,0:T(8,128)S(1)}, u32[]{:S(2)}, u32[]{:S(2)}) collective-permute-start(f32[512,256]{1,0:T(8,128)S(1)} %turn_lower.14), channel_id=1, source_target_pairs={{0,8},{1,9},{2,10},{3,11},{4,12},{5,13},{6,14},{7,15},{8,16},{9,17... | collective-permute-start | bytes 1572872 | tf_op jit(solution)/shard_map/ppermute | solution.py:234
  114.8 26.6 %collective-permute-start.13 = (f32[512,256]{1,0:T(8,128)S(1)}, f32[512,256]{1,0:T(8,128)S(1)}, u32[]{:S(2)}, u32[]{:S(2)}) collective-permute-start(f32[512,256]{1,0:T(8,128)S(1)} %turn_lower.15), channel_id=1, source_target_pairs={{0,8},{1,9},{2,10},{3,11},{4,12},{5,13},{6,14},{7,15},{8,16},{9,17... | collective-permute-start | bytes 1572872 | tf_op jit(solution)/shard_map/ppermute | solution.py:234

commit v2 on v1

v2 whole, which is shorter than its diff:
```python
import functools

import jax
import jax.numpy as jnp
from jax import lax
from jax.experimental import pallas as pl
from jax.experimental.pallas import tpu as pltpu
from jax.sharding import PartitionSpec as P

PIECES = 2
LAST_PIECES = 2
TAIL = 8
ROUNDS = (1, 2, 6)
F32 = jnp.float32
BF16 = jnp.bfloat16
PLAIN = (((1,), (0,)), ((), ()))
ROWS_FIRST = (((0,), (0,)), ((), ()))
COLS_LAST = (((1,), (1,)), ((), ()))
VMEM = pl.BlockSpec(memory_space=pltpu.VMEM)
MIB = 1 << 20


def halves(value):
    high = value.astype(BF16)
    return high, (value - high.astype(F32)).astype(BF16)


def dot(left, right, dims=PLAIN):
    return lax.dot_general(left, right, dims, preferred_element_type=F32)


def exact(left, right, dims=PLAIN):
    return lax.dot_general(
        left, right, dims, precision=lax.Precision.HIGHEST, preferred_element_type=F32
    )


def part_of(upper, lower):
    upper_high, upper_low = halves(upper)
    lower_high, lower_low = halves(lower)
    cross = dot(upper_high, lower_high, ROWS_FIRST)
    cross += dot(upper_high, lower_low, ROWS_FIRST)
    cross += dot(upper_low, lower_high, ROWS_FIRST)
    width = upper.shape[1]
    row = lax.broadcasted_iota(jnp.int32, (TAIL, width), 0)
    norms = jnp.where(row == 0, jnp.sum(upper * upper, axis=0, keepdims=True), 0.0)
    norms = jnp.where(row == 1, jnp.sum(lower * lower, axis=0, keepdims=True), norms)
    return cross, norms


def first_gram_body(tile, matrix_ref, out_ref, block_ref, sems):
    rows, width = block_ref.shape[0], out_ref.shape[1]
    copies = []
    for k in range(rows // tile):
        part = pl.ds(k * tile, tile)
        copies.append(
            pltpu.make_async_copy(matrix_ref.at[part, :], block_ref.at[part, :], sems.at[k])
        )
        copies[-1].start()
    total = None
    for k, copy in enumerate(copies):
        copy.wait()
        at = pl.ds(k * tile, tile)
        part = part_of(block_ref[at, :width], block_ref[at, width:])
        total = part if total is None else tuple(a + b for a, b in zip(total, part))
    out_ref[:width], out_ref[width:] = total


def first_gram(matrix, tile=512):
    rows, width = matrix.shape[0], matrix.shape[1] // 2
    return pl.pallas_call(
        functools.partial(first_gram_body, tile),
        in_specs=[pl.BlockSpec(memory_space=pltpu.HBM)],
        out_specs=(VMEM, VMEM),
        out_shape=(
            jax.ShapeDtypeStruct((width + TAIL, width), F32),
            jax.ShapeDtypeStruct(matrix.shape, F32),
        ),
        scratch_shapes=[pltpu.SemaphoreType.DMA((rows // tile,))],
        compiler_params=pltpu.CompilerParams(vmem_limit_bytes=16 * MIB),
        name="first_gram",
    )(matrix)


def gram_body(tile, count, upper_ref, *refs):
    lower_refs, out_ref = refs[:count], refs[-1]
    width = upper_ref.shape[1]
    start, total = 0, None
    for lower_ref in lower_refs:
        for at in range(0, lower_ref.shape[0], tile):
            part = part_of(upper_ref[pl.ds(start, tile), :], lower_ref[pl.ds(at, tile), :])
            total = part if total is None else tuple(a + b for a, b in zip(total, part))
            start += tile
    out_ref[:width], out_ref[width:] = total


def gram(upper, lowers, tile=512):
    width = upper.shape[1]
    return pl.pallas_call(
        functools.partial(gram_body, tile, len(lowers)),
        in_specs=[VMEM] * (1 + len(lowers)),
        out_specs=VMEM,
        out_shape=jax.ShapeDtypeStruct((width + TAIL, width), F32),
        compiler_params=pltpu.CompilerParams(vmem_limit_bytes=8 * MIB),
        name="gram",
    )(upper, *lowers)


def split_dot(left, right):
    return dot(left[0], right[0]) + (dot(left[0], right[1]) + dot(left[1], right[0]))


def solve_body(left_ref, right_ref, high_ref, low_ref, inverse_ref):
    width = left_ref.shape[1]
    cross = left_ref[:width] + right_ref[:width]
    norms = left_ref[width:] + right_ref[width:]
    row = lax.broadcasted_iota(jnp.int32, (width, width), 0)
    column = lax.broadcasted_iota(jnp.int32, (width, width), 1)
    identity = jnp.where(row == column, 1.0, 0.0).astype(F32)
    upper_norms = jnp.sum(jnp.where(row == column, norms[0:1], 0.0), axis=1, keepdims=True)
    damped = cross / (upper_norms + norms[1:2])
    square = exact(damped, damped, COLS_LAST)
    bound = jnp.max(jnp.sum(jnp.abs(square), axis=0))
    scale = 2.0 / (2.0 + bound)
    whole = identity + square
    rest = identity - scale * whole
    rest_halves = halves(rest)
    second = split_dot(rest_halves, rest_halves)
    third = split_dot(rest_halves, halves(second))
    inverse_ref[...] = scale * (identity + (rest + (second + third)))

    def more(state):
        count, off = state
        return jnp.logical_and(count < 40, off > 1e-3)

    def refine(state):
        count, _ = state
        inverse = inverse_ref[...]
        rest = identity - exact(whole, inverse)
        inverse_ref[...] = inverse + exact(inverse, rest)
        return count + 1, jnp.max(jnp.sum(jnp.abs(rest), axis=0))

    near_one = bound / (2.0 + bound)
    lax.while_loop(more, refine, (jnp.int32(0), near_one * near_one))
    inverse = inverse_ref[...]
    damped_halves = halves(damped)
    into_lower = 2.0 * split_dot(halves(inverse), damped_halves)
    into_upper = -into_lower.T
    into_upper_halves = halves(into_upper)
    keep_lower = identity + split_dot(into_upper_halves, damped_halves)
    for place, (high, low) in (
        ((0, 0), halves(2.0 * inverse - identity)),
        ((0, 1), halves(into_lower)),
        ((1, 0), into_upper_halves),
        ((1, 1), halves(keep_lower)),
    ):
        at = (pl.ds(place[0] * width, width), pl.ds(place[1] * width, width))
        high_ref[at] = high
        low_ref[at] = low


def solve(left, right):
    width = left.shape[1]
    out = jax.ShapeDtypeStruct((2 * width, 2 * width), BF16)
    return pl.pallas_call(
        solve_body,
        in_specs=[VMEM] * 2,
        out_specs=(VMEM, VMEM),
        out_shape=(out, out),
        scratch_shapes=[pltpu.VMEM((width, width), F32)],
        compiler_params=pltpu.CompilerParams(vmem_limit_bytes=8 * MIB),
        name="solve",
    )(left, right)


def turn_rows(block_refs, starts, high_ref, low_ref, side, at, tile):
    width = 256
    columns = pl.ds(side * width, width)
    total, depth = None, 0
    for ref, first in zip(block_refs, starts):
        high, low = halves(ref[pl.ds(first + at, tile), :])
        rows = pl.ds(depth, high.shape[1])
        turn_high, turn_low = high_ref[rows, columns], low_ref[rows, columns]
        part = dot(high, turn_high) + dot(low, turn_high) + dot(high, turn_low)
        total = part if total is None else total + part
        depth += high.shape[1]
    return total


def turn_body(side, starts, tile, *refs):
    *block_refs, high_ref, low_ref, out_ref = refs
    if starts is None:
        at = 0
        for lower_ref in block_refs[1:]:
            for inner in range(0, lower_ref.shape[0], tile):
                out_ref[pl.ds(at, tile), :] = turn_rows(
                    (block_refs[0], lower_ref), (at - inner, 0), high_ref, low_ref, side, inner, tile
                )
                at += tile
        return
    for at in range(0, out_ref.shape[0], tile):
        total = turn_rows(block_refs, starts, high_ref, low_ref, side, at, tile)
        out_ref[pl.ds(at, tile), :] = total


def turn(blocks, turns, side, starts, rows, tile=512):
    return pl.pallas_call(
        functools.partial(turn_body, side, starts, tile),
        in_specs=[VMEM] * (len(blocks) + 2),
        out_specs=VMEM,
        out_shape=jax.ShapeDtypeStruct((rows, 256), F32),
        compiler_params=pltpu.CompilerParams(vmem_limit_bytes=8 * MIB),
        name="turn_lower" if side else "turn_upper",
    )(*blocks, *turns)


def last_body(tile, count, flag_ref, done_ref, upper_ref, *refs):
    lower_refs, (high_ref, low_ref) = refs[:count], refs[count : count + 2]
    piece_refs, out_ref = refs[count + 2 : 2 * count + 2], refs[2 * count + 2]
    stage_ref, sem = refs[2 * count + 3 :]
    width = upper_ref.shape[1]
    columns = out_ref.at[:, pl.ds(0, width)]

    @pl.when(flag_ref[0] == 1)
    def _():
        fetch = pltpu.make_async_copy(done_ref, stage_ref, sem)
        fetch.start()
        fetch.wait()

    @pl.when(flag_ref[0] == 0)
    def _():
        at = 0
        for lower_ref, piece_ref in zip(lower_refs, piece_refs):
            for inner in range(0, lower_ref.shape[0], tile):
                blocks, starts = (upper_ref, lower_ref), (at - inner, 0)
                stage_ref[pl.ds(at, tile), :] = turn_rows(
                    blocks, starts, high_ref, low_ref, 0, inner, tile
                )
                piece_ref[pl.ds(inner, tile), :] = turn_rows(
                    blocks, starts, high_ref, low_ref, 1, inner, tile
                )
                at += tile

    copy = pltpu.make_async_copy(stage_ref, columns, sem)
    copy.start()
    copy.wait()


def last_turn(flag, done, upper, far, turns_far, tile=512):
    rows, width = upper.shape
    everywhere = pl.BlockSpec(memory_space=pl.ANY)
    *pieces, out = pl.pallas_call(
        functools.partial(last_body, tile, len(far)),
        in_specs=[pl.BlockSpec(memory_space=pltpu.SMEM)] + [VMEM] * (4 + len(far)),
        out_specs=(*[VMEM] * len(far), everywhere),
        out_shape=(
            *[jax.ShapeDtypeStruct(piece.shape, F32) for piece in far],
            jax.ShapeDtypeStruct((rows, 2 * width), F32),
        ),
        scratch_shapes=[pltpu.VMEM((rows, width), F32), pltpu.SemaphoreType.DMA],
        compiler_params=pltpu.CompilerParams(vmem_limit_bytes=8 * MIB),
        name="last_turn",
    )(flag, done, upper, *far, *turns_far)
    return pieces, out


def finish_body(count, flag_ref, before_ref, *refs):
    near_refs, far_refs, out_ref = refs[:count], refs[count : 2 * count], refs[2 * count]
    stage_ref, in_sems, out_sems = refs[2 * count + 1 :]
    width = stage_ref.shape[1]
    for want, sources in ((1, near_refs), (0, far_refs)):

        @pl.when(flag_ref[0] == want)
        def _(sources=sources):
            at, spans, fetches, puts = 0, [], [], []
            for k, source in enumerate(sources):
                spans.append(pl.ds(at, source.shape[0]))
                fetches.append(
                    pltpu.make_async_copy(source, stage_ref.at[spans[k], :], in_sems.at[k])
                )
                fetches[k].start()
                at += source.shape[0]
            for k, span in enumerate(spans):
                fetches[k].wait()
                place = out_ref.at[span, pl.ds(width, width)]
                puts.append(pltpu.make_async_copy(stage_ref.at[span, :], place, out_sems.at[k]))
                puts[k].start()
            for put in puts:
                put.wait()


def finish(flag, out, near, far):
    rows, width = out.shape[0], out.shape[1] // 2
    everywhere = pl.BlockSpec(memory_space=pl.ANY)
    count = len(near)
    return pl.pallas_call(
        functools.partial(finish_body, count),
        in_specs=[pl.BlockSpec(memory_space=pltpu.SMEM)] + [everywhere] * (1 + 2 * count),
        out_specs=everywhere,
        out_shape=jax.ShapeDtypeStruct(out.shape, F32),
        scratch_shapes=[
            pltpu.VMEM((rows, width), F32),
            pltpu.SemaphoreType.DMA((count,)),
            pltpu.SemaphoreType.DMA((count,)),
        ],
        input_output_aliases={1: 0},
        compiler_params=pltpu.CompilerParams(vmem_limit_bytes=8 * MIB),
        name="finish",
    )(flag, out, *near, *far)


def move(value, target):
    wide, narrow = lax.axis_size("wide"), lax.axis_size("narrow")
    pairs = []
    for w in range(wide):
        for n in range(narrow):
            to = target(w, n)
            if to is not None:
                pairs.append((w * narrow + n, (to[0] % wide) * narrow + to[1]))
    return lax.ppermute(value, ("wide", "narrow"), pairs)


def all_sum(value, active=None, rounds=ROUNDS):
    for k, mask in enumerate(rounds):
        other = move(
            value, lambda w, n: (w, n ^ mask if active is None or w % 2 == active else n)
        )
        if k + 1 == len(rounds):
            return value, other
        value = value + other


def within(w, n):
    return w ^ 1, n


def onward(w, n):
    return w + 1, n


def shards(matrix):
    rows = matrix.shape[0]
    piece, small = rows // PIECES, rows // LAST_PIECES
    starts = [k * piece for k in range(PIECES)]
    last_starts = [k * small for k in range(LAST_PIECES)]
    flag = (lax.axis_index("wide") & 1).astype(jnp.int32).reshape(1)
    parts, matrix = first_gram(matrix)
    turns = solve(*all_sum(parts))
    near, far = [], []
    for at in starts:
        lower = turn([matrix], turns, 1, (at,), piece)
        near.append(move(lower, within))
        far.append(move(lower, onward))
    upper = turn([matrix], turns, 0, (0,), rows)
    turns = solve(*all_sum(gram(upper, near), 1, (2, 6, 1)))
    after = [
        turn([upper, near[at // piece]], turns, 1, (at, at % piece), small)
        for at in last_starts
    ]
    done = turn([upper, *near], turns, 0, None, rows)
    last_far = [move(lower, onward) for lower in after]
    parts = gram(upper, far)
    parts = parts + move(parts, lambda w, n: (w, n if w % 2 else n ^ 1))
    parts = all_sum(parts, 0, (2, 6))
    turns = solve(*parts)
    pieces, out = last_turn(flag, done, upper, far, turns)
    last_near = [move(lower, within) for lower in pieces]
    return finish(flag, out, last_near, last_far)


def solution(mesh):
    spec = P("narrow", "wide")

    return jax.shard_map(shards, mesh=mesh, in_specs=(spec,), out_specs=spec, check_vma=False)
```

time: 143 us -> 174 us (1.22)
  Pallas kernels: 43.4 us -> 65.1 us
  starting transfers between devices: 17.6 us -> 24.5 us
  waiting for transfers between devices: 75.5 us -> 78.4 us
    pallas_call x2 -> x3, Pallas kernels: 30.1 us -> 46.3 us  [solve(): pl.pallas_call(solve_body, in_specs=[VMEM] * 2, out_specs=(VMEM, VMEM), o...]
    ppermute x14 -> x17, starting transfers between devices: 17.6 us -> 24.5 us  [move(): return lax.ppermute(value, ('wide', 'narrow'), pairs)]
    dynamic_update_slice x4 -> x0, local copies, waits for them, and re-layouts: 3.31 us -> none  [shards(): out = lax.dynamic_update_slice(out, last[k], (at, width))]
    pallas_call x2 -> x3, Pallas kernels: 5.64 us -> 8.77 us  [the longest x1 4.77 us: last_turn(): pl.pallas_call(functools.partial(last_body, tile, len(far)), in_specs=[pl...]
    ppermute x14 -> x17, waiting for transfers between devices: 75.5 us -> 78.4 us  [move(): return lax.ppermute(value, ('wide', 'narrow'), pairs)]
    unnamed x4 -> x14, local copies, waits for them, and re-layouts: 2.19 us -> 4.39 us
    pallas_call x9 -> x6, Pallas kernels: 6.43 us -> 7.55 us  [turn(): pl.pallas_call(functools.partial(turn_body, side, starts, tile), in_specs...]
  transfers between devices with their start and end apart: 14 -> 17, of which waited for: 14 -> 11; matrix products, arithmetic and copies ran while one was open for 2% -> 0% of each run, Pallas kernels for 5% -> 12%
where the time goes in v2:
time: 174 us
  waiting for transfers between devices  78.4 us (45%)
  Pallas kernels  65.1 us (37%)
  starting transfers between devices  24.5 us (14%)
  local copies, waits for them, and re-layouts  4.39 us (3%)
    ppermute x17, waiting for transfers between devices, move(): return lax.ppermute(value, ('wide', 'narrow'), pairs)  78.4 us
    pallas_call x3, Pallas kernels, solve(): pl.pallas_call(solve_body, in_specs=[VMEM] * 2, out_specs=(VMEM, VMEM), o...  46.3 us
    ppermute x17, starting transfers between devices, move(): return lax.ppermute(value, ('wide', 'narrow'), pairs)  24.5 us
    pallas_call x6, Pallas kernels, turn(): pl.pallas_call(functools.partial(turn_body, side, starts, tile), in_specs...  7.55 us
    pallas_call x1, Pallas kernels, last_turn(): pl.pallas_call(functools.partial(last_body, tile, len(far)), in_specs=[pl...  4.77 us
    unnamed x14, local copies, waits for them, and re-layouts  4.39 us
  transfers between devices with their start and end apart: 17, of which 11 were waited for; matrix products, arithmetic and copies ran while one was open for 0% of the time, Pallas kernels for 12%

profile of v2, /device:TPU:16, one launch (start us, length us, event | category | flops | bytes accessed | tf_op | source)
XLA Modules:
  0.0 173.7 jit_solution(1580186461096645261)
XLA Ops:
  0.0 2.2 %copy-done.2 = f32[2048,512]{1,0:T(8,128)S(1)} copy-done((f32[2048,512]{1,0:T(8,128)S(1)}, f32[2048,512]{1,0:T(8,128)}, u32[]{:S(2)}) %copy-start.2) | copy-done | bytes 4194328
  2.2 2.5 %first_gram.1 = (f32[264,256]{1,0:T(8,128)S(1)}, f32[2048,512]{1,0:T(8,128)S(1)}) custom-call(f32[2048,512]{1,0:T(8,128)S(1)} %copy-done.2), custom_call_target="tpu_custom_call" | custom-call | tf_op jit(solution)/shard_map/first_gram/pallas_call | solution.py:71
  6.1 6.9 %collective-permute-done = f32[264,256]{1,0:T(8,128)S(1)} collective-permute-done((f32[264,256]{1,0:T(8,128)S(1)}, f32[264,256]{1,0:T(8,128)S(1)}, u32[]{:S(2)}, u32[]{:S(2)}) %collective-permute-start) | collective-permute-done | bytes 270368 | tf_op jit(solution)/shard_map/ppermute | solution.py:320
  13.1 1.6 collective-permute-start.1
  14.6 5.9 %collective-permute-done.1 = f32[264,256]{1,0:T(8,128)S(1)} collective-permute-done((f32[264,256]{1,0:T(8,128)S(1)}, f32[264,256]{1,0:T(8,128)S(1)}, u32[]{:S(2)}, u32[]{:S(2)}) %collective-permute-start.1) | collective-permute-done | bytes 270368 | tf_op jit(solution)/shard_map/ppermute | solution.py:320
  20.5 2.8 %collective-permute-start.2 = (f32[264,256]{1,0:T(8,128)S(1)}, f32[264,256]{1,0:T(8,128)S(1)}, u32[]{:S(2)}, u32[]{:S(2)}) collective-permute-start(f32[264,256]{1,0:T(8,128)S(1)} %add.19.left_ref), channel_id=1, source_target_pairs={{0,6},{1,7},{2,4},{3,5},{4,2},{5,3},{6,0},{7,1},{8,14},{9,15},{10,... | collective-permute-start | bytes 811016 | tf_op jit(solution)/shard_map/ppermute | solution.py:320
  23.4 5.0 %collective-permute-done.2.right_ref = f32[264,256]{1,0:T(8,128)S(1)} collective-permute-done((f32[264,256]{1,0:T(8,128)S(1)}, f32[264,256]{1,0:T(8,128)S(1)}, u32[]{:S(2)}, u32[]{:S(2)}) %collective-permute-start.2) | collective-permute-done | bytes 270368 | tf_op jit(solution)/shard_map/ppermute | solution.py:320
  28.4 14.4 %solve.3 = (bf16[512,512]{1,0:T(8,128)(2,1)S(1)}, bf16[512,512]{1,0:T(8,128)(2,1)S(1)}) custom-call(f32[264,256]{1,0:T(8,128)S(1)} %add.19.left_ref, f32[264,256]{1,0:T(8,128)S(1)} %collective-permute-done.2.right_ref), custom_call_target="tpu_custom_call" | custom-call | tf_op jit(solution)/shard_map/solve/pallas_call | solution.py:165
  44.8 2.0 %collective-permute-start.9 = (f32[1024,256]{1,0:T(8,128)S(1)}, f32[1024,256]{1,0:T(8,128)S(1)}, u32[]{:S(2)}, u32[]{:S(2)}) collective-permute-start(f32[1024,256]{1,0:T(8,128)S(1)} %turn_lower.5), channel_id=1, source_target_pairs={{0,8},{1,9},{2,10},{3,11},{4,12},{5,13},{6,14},{7,15},{8,16},{9,17... | collective-permute-start | bytes 3145736 | tf_op jit(solution)/shard_map/ppermute | solution.py:320
  47.4 1.8 %turn_upper.2.upper_ref.refs_0_ = f32[2048,256]{1,0:T(8,128)S(1)} custom-call(f32[2048,512]{1,0:T(8,128)S(1)} %get-tuple-element.16.refs_0_, bf16[512,512]{1,0:T(8,128)(2,1)S(1)} %get-tuple-element.18.refs_1_, bf16[512,512]{1,0:T(8,128)(2,1)S(1)} %get-tuple-element.19.refs_2_), custom_call_target="tpu_custom_call" | custom-call | tf_op jit(solution)/shard_map/turn_upper/pallas_call | solution.py:207
  49.2 13.5 %collective-permute-done.8.refs_0_ = f32[1024,256]{1,0:T(8,128)S(1)} collective-permute-done((f32[1024,256]{1,0:T(8,128)S(1)}, f32[1024,256]{1,0:T(8,128)S(1)}, u32[]{:S(2)}, u32[]{:S(2)}) %collective-permute-start.8) | collective-permute-done | bytes 1048608 | tf_op jit(solution)/shard_map/ppermute | solution.py:320
  62.6 11.2 %collective-permute-done.9.refs_1_ = f32[1024,256]{1,0:T(8,128)S(1)} collective-permute-done((f32[1024,256]{1,0:T(8,128)S(1)}, f32[1024,256]{1,0:T(8,128)S(1)}, u32[]{:S(2)}, u32[]{:S(2)}) %collective-permute-start.9) | collective-permute-done | bytes 1048608 | tf_op jit(solution)/shard_map/ppermute | solution.py:320
  75.2 3.4 %collective-permute-start.10 = (f32[264,256]{1,0:T(8,128)S(1)}, f32[264,256]{1,0:T(8,128)S(1)}, u32[]{:S(2)}, u32[]{:S(2)}) collective-permute-start(f32[264,256]{1,0:T(8,128)S(1)} %gram.3), channel_id=1, source_target_pairs={{0,1},{1,0},{2,3},{3,2},{4,5},{5,4},{6,7},{7,6},{8,8},{9,9},{10,10... | collective-permute-start | bytes 811016 | tf_op jit(solution)/shard_map/ppermute | solution.py:320
  81.5 2.0 %collective-permute-done.10 = f32[264,256]{1,0:T(8,128)S(1)} collective-permute-done((f32[264,256]{1,0:T(8,128)S(1)}, f32[264,256]{1,0:T(8,128)S(1)}, u32[]{:S(2)}, u32[]{:S(2)}) %collective-permute-start.10) | collective-permute-done | bytes 270368 | tf_op jit(solution)/shard_map/ppermute | solution.py:320
  83.6 2.2 %collective-permute-start.11 = (f32[264,256]{1,0:T(8,128)S(1)}, f32[264,256]{1,0:T(8,128)S(1)}, u32[]{:S(2)}, u32[]{:S(2)}) collective-permute-start(f32[264,256]{1,0:T(8,128)S(1)} %add.22), channel_id=1, source_target_pairs={{0,2},{1,3},{2,0},{3,1},{4,6},{5,7},{6,4},{7,5},{8,8},{9,9},{10,10... | collective-permute-start | bytes 811016 | tf_op jit(solution)/shard_map/ppermute | solution.py:320
  86.5 5.4 %collective-permute-done.11 = f32[264,256]{1,0:T(8,128)S(1)} collective-permute-done((f32[264,256]{1,0:T(8,128)S(1)}, f32[264,256]{1,0:T(8,128)S(1)}, u32[]{:S(2)}, u32[]{:S(2)}) %collective-permute-start.11) | collective-permute-done | bytes 270368 | tf_op jit(solution)/shard_map/ppermute | solution.py:320
  91.9 4.7 %collective-permute-start.12 = (f32[264,256]{1,0:T(8,128)S(1)}, f32[264,256]{1,0:T(8,128)}, u32[]{:S(2)}, u32[]{:S(2)}) collective-permute-start(f32[264,256]{1,0:T(8,128)S(1)} %add.23.left_ref), channel_id=1, source_target_pairs={{0,6},{1,7},{2,4},{3,5},{4,2},{5,3},{6,0},{7,1},{8,8},{9,9},{10,10... | collective-permute-start | bytes 811016 | tf_op jit(solution)/shard_map/ppermute | solution.py:320
  97.4 3.7 %collective-permute-start.7 = (f32[264,256]{1,0:T(8,128)}, f32[264,256]{1,0:T(8,128)}, u32[]{:S(2)}, u32[]{:S(2)}) collective-permute-start(f32[264,256]{1,0:T(8,128)} %add.21.left_ref), channel_id=1, source_target_pairs={{0,0},{1,1},{2,2},{3,3},{4,4},{5,5},{6,6},{7,7},{8,9},{9,8},{10,11... | collective-permute-start | bytes 811016 | tf_op jit(solution)/shard_map/ppermute | solution.py:320
  101.6 15.3 %solve.5 = (bf16[512,512]{1,0:T(8,128)(2,1)S(1)}, bf16[512,512]{1,0:T(8,128)(2,1)S(1)}) custom-call(f32[264,256]{1,0:T(8,128)S(1)} %add.23.left_ref, f32[264,256]{1,0:T(8,128)} %collective-permute-done.12.right_ref), custom_call_target="tpu_custom_call" | custom-call | tf_op jit(solution)/shard_map/solve/pallas_call | solution.py:165
  117.0 16.5 %solve.4 = (bf16[512,512]{1,0:T(8,128)(2,1)S(1)}, bf16[512,512]{1,0:T(8,128)(2,1)S(1)}) custom-call(f32[264,256]{1,0:T(8,128)} %add.21.left_ref, f32[264,256]{1,0:T(8,128)} %collective-permute-done.7.right_ref), custom_call_target="tpu_custom_call" | custom-call | tf_op jit(solution)/shard_map/solve/pallas_call | solution.py:165
  134.8 1.8 %turn_upper.3.done_ref = f32[2048,256]{1,0:T(8,128)S(1)} custom-call(f32[2048,256]{1,0:T(8,128)S(1)} %turn_upper.2.upper_ref.refs_0_, f32[1024,256]{1,0:T(8,128)S(1)} %copy-done.1, f32[1024,256]{1,0:T(8,128)S(1)} %collective-permute-done.4.refs_1_.refs_2_, bf16[512,512]{1,0:T(8,128)(2,1)S(1)} %get-tuple-element.20.refs_3_.refs_2_, ...), custom_call_target="tpu_custom_call" | custom-call | tf_op jit(solution)/shard_map/turn_upper/pallas_call | solution.py:207
  136.6 4.8 %last_turn.1 = (f32[1024,256]{1,0:T(8,128)S(1)}, f32[1024,256]{1,0:T(8,128)S(1)}, f32[2048,512]{1,0:T(8,128)}) custom-call(s32[1]{0:T(128)} %bitcast.flag_ref, f32[2048,256]{1,0:T(8,128)S(1)} %turn_upper.3.done_ref, f32[2048,256]{1,0:T(8,128)S(1)} %turn_upper.2.upper_ref.refs_0_, f32[1024,256]{1,0:T(8,128)S(1)} %copy-done.4, f32[1024,256]{1,0:T(8,128)S(1)} %copy-done.6, ...), custom_call_target="tpu_custom_call" | custom-call | tf_op jit(solution)/shard_map/last_turn/pallas_call | solution.py:252
  145.6 15.3 %collective-permute-done.15.refs_2_ = f32[1024,256]{1,0:T(8,128)S(1)} collective-permute-done((f32[1024,256]{1,0:T(8,128)S(1)}, f32[1024,256]{1,0:T(8,128)S(1)}, u32[]{:S(2)}, u32[]{:S(2)}) %collective-permute-start.15) | collective-permute-done | bytes 1048608 | tf_op jit(solution)/shard_map/ppermute | solution.py:320
  160.9 11.2 %collective-permute-done.16.refs_3_ = f32[1024,256]{1,0:T(8,128)S(1)} collective-permute-done((f32[1024,256]{1,0:T(8,128)S(1)}, f32[1024,256]{1,0:T(8,128)S(1)}, u32[]{:S(2)}, u32[]{:S(2)}) %collective-permute-start.16) | collective-permute-done | bytes 1048608 | tf_op jit(solution)/shard_map/ppermute | solution.py:320
  (44 shorter events, 17.2 us)
Async XLA Ops:
  0.0 2.2 %copy-start.2 = (f32[2048,512]{1,0:T(8,128)S(1)}, f32[2048,512]{1,0:T(8,128)}, u32[]{:S(2)}) copy-start(f32[2048,512]{1,0:T(8,128)} %matrix_ref.1) | copy-start | bytes 12582916
  4.7 8.3 %collective-permute-start = (f32[264,256]{1,0:T(8,128)S(1)}, f32[264,256]{1,0:T(8,128)S(1)}, u32[]{:S(2)}, u32[]{:S(2)}) collective-permute-start(f32[264,256]{1,0:T(8,128)S(1)} %get-tuple-element.17), channel_id=1, source_target_pairs={{0,1},{1,0},{2,3},{3,2},{4,5},{5,4},{6,7},{7,6},{8,9},{9,8},{10,11... | collective-permute-start | bytes 811016 | tf_op jit(solution)/shard_map/ppermute | solution.py:320
  13.1 7.5 %collective-permute-start.1 = (f32[264,256]{1,0:T(8,128)S(1)}, f32[264,256]{1,0:T(8,128)S(1)}, u32[]{:S(2)}, u32[]{:S(2)}) collective-permute-start(f32[264,256]{1,0:T(8,128)S(1)} %add.18), channel_id=1, source_target_pairs={{0,2},{1,3},{2,0},{3,1},{4,6},{5,7},{6,4},{7,5},{8,10},{9,11},{10,... | collective-permute-start | bytes 811016 | tf_op jit(solution)/shard_map/ppermute | solution.py:320
  20.5 7.8 %collective-permute-start.2 = (f32[264,256]{1,0:T(8,128)S(1)}, f32[264,256]{1,0:T(8,128)S(1)}, u32[]{:S(2)}, u32[]{:S(2)}) collective-permute-start(f32[264,256]{1,0:T(8,128)S(1)} %add.19.left_ref), channel_id=1, source_target_pairs={{0,6},{1,7},{2,4},{3,5},{4,2},{5,3},{6,0},{7,1},{8,14},{9,15},{10,... | collective-permute-start | bytes 811016 | tf_op jit(solution)/shard_map/ppermute | solution.py:320
  44.7 17.9 %collective-permute-start.8 = (f32[1024,256]{1,0:T(8,128)S(1)}, f32[1024,256]{1,0:T(8,128)S(1)}, u32[]{:S(2)}, u32[]{:S(2)}) collective-permute-start(f32[1024,256]{1,0:T(8,128)S(1)} %turn_lower.4), channel_id=1, source_target_pairs={{0,8},{1,9},{2,10},{3,11},{4,12},{5,13},{6,14},{7,15},{8,16},{9,17... | collective-permute-start | bytes 3145736 | tf_op jit(solution)/shard_map/ppermute | solution.py:320
  44.8 29.1 %collective-permute-start.9 = (f32[1024,256]{1,0:T(8,128)S(1)}, f32[1024,256]{1,0:T(8,128)S(1)}, u32[]{:S(2)}, u32[]{:S(2)}) collective-permute-start(f32[1024,256]{1,0:T(8,128)S(1)} %turn_lower.5), channel_id=1, source_target_pairs={{0,8},{1,9},{2,10},{3,11},{4,12},{5,13},{6,14},{7,15},{8,16},{9,17... | collective-permute-start | bytes 3145736 | tf_op jit(solution)/shard_map/ppermute | solution.py:320
  46.8 31.7 %collective-permute-start.3 = (f32[1024,256]{1,0:T(8,128)S(1)}, f32[1024,256]{1,0:T(8,128)S(1)}, u32[]{:S(2)}, u32[]{:S(2)}) collective-permute-start(f32[1024,256]{1,0:T(8,128)S(1)} %turn_lower.4), channel_id=1, source_target_pairs={{0,8},{1,9},{2,10},{3,11},{4,12},{5,13},{6,14},{7,15},{8,0},{9,1},... | collective-permute-start | bytes 3145736 | tf_op jit(solution)/shard_map/ppermute | solution.py:320
  46.9 31.6 %collective-permute-start.4 = (f32[1024,256]{1,0:T(8,128)S(1)}, f32[1024,256]{1,0:T(8,128)S(1)}, u32[]{:S(2)}, u32[]{:S(2)}) collective-permute-start(f32[1024,256]{1,0:T(8,128)S(1)} %turn_lower.5), channel_id=1, source_target_pairs={{0,8},{1,9},{2,10},{3,11},{4,12},{5,13},{6,14},{7,15},{8,0},{9,1},... | collective-permute-start | bytes 3145736 | tf_op jit(solution)/shard_map/ppermute | solution.py:320
  62.6 17.2 %copy-start.3 = (f32[1024,256]{1,0:T(8,128)}, f32[1024,256]{1,0:T(8,128)S(1)}, u32[]{:S(2)}) copy-start(f32[1024,256]{1,0:T(8,128)S(1)} %collective-permute-done.8.refs_0_) | copy-start | bytes 3145732
  73.9 5.9 %copy-start.5 = (f32[1024,256]{1,0:T(8,128)}, f32[1024,256]{1,0:T(8,128)S(1)}, u32[]{:S(2)}) copy-start(f32[1024,256]{1,0:T(8,128)S(1)} %collective-permute-done.9.refs_1_) | copy-start | bytes 3145732
  75.2 8.4 %collective-permute-start.10 = (f32[264,256]{1,0:T(8,128)S(1)}, f32[264,256]{1,0:T(8,128)S(1)}, u32[]{:S(2)}, u32[]{:S(2)}) collective-permute-start(f32[264,256]{1,0:T(8,128)S(1)} %gram.3), channel_id=1, source_target_pairs={{0,1},{1,0},{2,3},{3,2},{4,5},{5,4},{6,7},{7,6},{8,8},{9,9},{10,10... | collective-permute-start | bytes 811016 | tf_op jit(solution)/shard_map/ppermute | solution.py:320
  79.8 1.0 copy-start
  80.8 5.0 %collective-permute-start.5 = (f32[264,256]{1,0:T(8,128)S(1)}, f32[264,256]{1,0:T(8,128)S(1)}, u32[]{:S(2)}, u32[]{:S(2)}) collective-permute-start(f32[264,256]{1,0:T(8,128)S(1)} %gram.2), channel_id=1, source_target_pairs={{0,0},{1,1},{2,2},{3,3},{4,4},{5,5},{6,6},{7,7},{8,10},{9,11},{10,... | collective-permute-start | bytes 811016 | tf_op jit(solution)/shard_map/ppermute | solution.py:320
  83.6 8.4 %collective-permute-start.11 = (f32[264,256]{1,0:T(8,128)S(1)}, f32[264,256]{1,0:T(8,128)S(1)}, u32[]{:S(2)}, u32[]{:S(2)}) collective-permute-start(f32[264,256]{1,0:T(8,128)S(1)} %add.22), channel_id=1, source_target_pairs={{0,2},{1,3},{2,0},{3,1},{4,6},{5,7},{6,4},{7,5},{8,8},{9,9},{10,10... | collective-permute-start | bytes 811016 | tf_op jit(solution)/shard_map/ppermute | solution.py:320
  85.8 10.8 %collective-permute-start.6 = (f32[264,256]{1,0:T(8,128)S(1)}, f32[264,256]{1,0:T(8,128)S(1)}, u32[]{:S(2)}, u32[]{:S(2)}) collective-permute-start(f32[264,256]{1,0:T(8,128)S(1)} %add.20), channel_id=1, source_target_pairs={{0,0},{1,1},{2,2},{3,3},{4,4},{5,5},{6,6},{7,7},{8,14},{9,15},{10,... | collective-permute-start | bytes 811016 | tf_op jit(solution)/shard_map/ppermute | solution.py:320
  91.9 9.7 %collective-permute-start.12 = (f32[264,256]{1,0:T(8,128)S(1)}, f32[264,256]{1,0:T(8,128)}, u32[]{:S(2)}, u32[]{:S(2)}) collective-permute-start(f32[264,256]{1,0:T(8,128)S(1)} %add.23.left_ref), channel_id=1, source_target_pairs={{0,6},{1,7},{2,4},{3,5},{4,2},{5,3},{6,0},{7,1},{8,8},{9,9},{10,10... | collective-permute-start | bytes 811016 | tf_op jit(solution)/shard_map/ppermute | solution.py:320
  97.4 19.6 %collective-permute-start.7 = (f32[264,256]{1,0:T(8,128)}, f32[264,256]{1,0:T(8,128)}, u32[]{:S(2)}, u32[]{:S(2)}) collective-permute-start(f32[264,256]{1,0:T(8,128)} %add.21.left_ref), channel_id=1, source_target_pairs={{0,0},{1,1},{2,2},{3,3},{4,4},{5,5},{6,6},{7,7},{8,9},{9,8},{10,11... | collective-permute-start | bytes 811016 | tf_op jit(solution)/shard_map/ppermute | solution.py:320
  101.1 35.5 %copy-start.4 = (f32[1024,256]{1,0:T(8,128)S(1)}, f32[1024,256]{1,0:T(8,128)}, u32[]{:S(2)}) copy-start(f32[1024,256]{1,0:T(8,128)} %copy-done.3) | copy-start | bytes 3145732
  133.5 1.2 copy-start.1
  134.7 1.8 %copy-start.6 = (f32[1024,256]{1,0:T(8,128)S(1)}, f32[1024,256]{1,0:T(8,128)}, u32[]{:S(2)}) copy-start(f32[1024,256]{1,0:T(8,128)} %copy-done.5) | copy-start | bytes 3145732
  141.4 2.9 %collective-permute-start.13 = (f32[1024,256]{1,0:T(8,128)S(1)}, f32[1024,256]{1,0:T(8,128)S(1)}, u32[]{:S(2)}, u32[]{:S(2)}) collective-permute-start(f32[1024,256]{1,0:T(8,128)S(1)} %get-tuple-element.25), channel_id=1, source_target_pairs={{0,8},{1,9},{2,10},{3,11},{4,12},{5,13},{6,14},{7,15},{8,0},{9,1},... | collective-permute-start | bytes 3145736 | tf_op jit(solution)/shard_map/ppermute | solution.py:320
  141.5 4.1 %collective-permute-start.14 = (f32[1024,256]{1,0:T(8,128)S(1)}, f32[1024,256]{1,0:T(8,128)S(1)}, u32[]{:S(2)}, u32[]{:S(2)}) collective-permute-start(f32[1024,256]{1,0:T(8,128)S(1)} %get-tuple-element.26), channel_id=1, source_target_pairs={{0,8},{1,9},{2,10},{3,11},{4,12},{5,13},{6,14},{7,15},{8,0},{9,1},... | collective-permute-start | bytes 3145736 | tf_op jit(solution)/shard_map/ppermute | solution.py:320
  142.9 17.9 %collective-permute-start.15 = (f32[1024,256]{1,0:T(8,128)S(1)}, f32[1024,256]{1,0:T(8,128)S(1)}, u32[]{:S(2)}, u32[]{:S(2)}) collective-permute-start(f32[1024,256]{1,0:T(8,128)S(1)} %turn_lower.6), channel_id=1, source_target_pairs={{0,8},{1,9},{2,10},{3,11},{4,12},{5,13},{6,14},{7,15},{8,16},{9,17... | collective-permute-start | bytes 3145736 | tf_op jit(solution)/shard_map/ppermute | solution.py:320
  144.1 28.0 %collective-permute-start.16 = (f32[1024,256]{1,0:T(8,128)S(1)}, f32[1024,256]{1,0:T(8,128)S(1)}, u32[]{:S(2)}, u32[]{:S(2)}) collective-permute-start(f32[1024,256]{1,0:T(8,128)S(1)} %turn_lower.7), channel_id=1, source_target_pairs={{0,8},{1,9},{2,10},{3,11},{4,12},{5,13},{6,14},{7,15},{8,16},{9,17... | collective-permute-start | bytes 3145736 | tf_op jit(solution)/shard_map/ppermute | solution.py:320

commit v3 on v2

--- a/solution.py
+++ b/solution.py
@@ -48,38 +48,35 @@
     return cross, norms
 
 
-def first_gram_body(tile, matrix_ref, out_ref, block_ref, sems):
-    rows, width = block_ref.shape[0], out_ref.shape[1]
-    copies = []
-    for k in range(rows // tile):
-        part = pl.ds(k * tile, tile)
-        copies.append(
-            pltpu.make_async_copy(matrix_ref.at[part, :], block_ref.at[part, :], sems.at[k])
-        )
-        copies[-1].start()
-    total = None
-    for k, copy in enumerate(copies):
-        copy.wait()
-        at = pl.ds(k * tile, tile)
-        part = part_of(block_ref[at, :width], block_ref[at, width:])
-        total = part if total is None else tuple(a + b for a, b in zip(total, part))
-    out_ref[:width], out_ref[width:] = total
-
-
-def first_gram(matrix, tile=512):
+def first_gram_body(upper_ref, lower_ref, out_ref):
+    width = upper_ref.shape[1]
+    cross, norms = part_of(upper_ref[...], lower_ref[...])
+
+    @pl.when(pl.program_id(0) == 0)
+    def _():
+        out_ref[:width] = cross
+        out_ref[width:] = norms
+
+    @pl.when(pl.program_id(0) > 0)
+    def _():
+        out_ref[:width] += cross
+        out_ref[width:] += norms
+
+
+def first_gram(matrix, tile=1024):
     rows, width = matrix.shape[0], matrix.shape[1] // 2
     return pl.pallas_call(
-        functools.partial(first_gram_body, tile),
-        in_specs=[pl.BlockSpec(memory_space=pltpu.HBM)],
-        out_specs=(VMEM, VMEM),
-        out_shape=(
-            jax.ShapeDtypeStruct((width + TAIL, width), F32),
-            jax.ShapeDtypeStruct(matrix.shape, F32),
-        ),
-        scratch_shapes=[pltpu.SemaphoreType.DMA((rows // tile,))],
-        compiler_params=pltpu.CompilerParams(vmem_limit_bytes=16 * MIB),
+        first_gram_body,
+        grid=(rows // tile,),
+        in_specs=[
+            pl.BlockSpec((tile, width), lambda i: (i, 0)),
+            pl.BlockSpec((tile, width), lambda i: (i, 1)),
+        ],
+        out_specs=pl.BlockSpec((width + TAIL, width), lambda i: (0, 0)),
+        out_shape=jax.ShapeDtypeStruct((width + TAIL, width), F32),
+        compiler_params=pltpu.CompilerParams(vmem_limit_bytes=8 * MIB),
         name="first_gram",
-    )(matrix)
+    )(matrix, matrix)
 
 
 def gram_body(tile, count, upper_ref, *refs):
@@ -344,8 +341,7 @@
     starts = [k * piece for k in range(PIECES)]
     last_starts = [k * small for k in range(LAST_PIECES)]
     flag = (lax.axis_index("wide") & 1).astype(jnp.int32).reshape(1)
-    parts, matrix = first_gram(matrix)
-    turns = solve(*all_sum(parts))
+    turns = solve(*all_sum(first_gram(matrix)))
     near, far = [], []
     for at in starts:
         lower = turn([matrix], turns, 1, (at,), piece)
@@ -361,7 +357,7 @@
     last_far = [move(lower, onward) for lower in after]
     parts = gram(upper, far)
     parts = parts + move(parts, lambda w, n: (w, n if w % 2 else n ^ 1))
-    parts = all_sum(parts, 0, (2, 6))
+    parts = all_sum(parts, None, (2, 6))
     turns = solve(*parts)
     pieces, out = last_turn(flag, done, upper, far, turns)
     last_near = [move(lower, within) for lower in pieces]

time: 174 us -> 170 us (0.977)
  starting transfers between devices: 24.5 us -> 20.8 us
    ppermute x17, starting transfers between devices: 24.5 us -> 20.8 us  [move(): return lax.ppermute(value, ('wide', 'narrow'), pairs)]
    unnamed x14 -> x16, local copies, waits for them, and re-layouts: 4.39 us -> 4.39 us
  transfers between devices with their start and end apart: 17 -> 17, of which waited for: 11 -> 11; matrix products, arithmetic and copies ran while one was open for 0% -> 0% of each run, Pallas kernels for 12% -> 13%
where the time goes in v3:
time: 170 us; the launch traced here: 169 us
  waiting for transfers between devices  78.5 us (46%)
  Pallas kernels  64.4 us (38%)
  starting transfers between devices  20.8 us (12%)
  local copies, waits for them, and re-layouts  4.39 us (3%)
    ppermute x17, waiting for transfers between devices, move(): return lax.ppermute(value, ('wide', 'narrow'), pairs)  78.5 us
    pallas_call x3, Pallas kernels, solve(): pl.pallas_call(solve_body, in_specs=[VMEM] * 2, out_specs=(VMEM, VMEM), o...  46.3 us
    ppermute x17, starting transfers between devices, move(): return lax.ppermute(value, ('wide', 'narrow'), pairs)  20.8 us
    pallas_call x6, Pallas kernels, turn(): pl.pallas_call(functools.partial(turn_body, side, starts, tile), in_specs...  7.55 us
    pallas_call x1, Pallas kernels, last_turn(): pl.pallas_call(functools.partial(last_body, tile, len(far)), in_specs=[pl...  4.77 us
    unnamed x16, local copies, waits for them, and re-layouts  4.39 us
  transfers between devices with their start and end apart: 17, of which 11 were waited for; matrix products, arithmetic and copies ran while one was open for 0% of the time, Pallas kernels for 13%

profile of v3, /device:TPU:16, one launch (start us, length us, event | category | flops | bytes accessed | tf_op | source)
XLA Modules:
  0.0 169.4 jit_solution(11232452906071351038)
XLA Ops:
  0.0 2.2 %copy-done = f32[2048,512]{1,0:T(8,128)S(1)} copy-done((f32[2048,512]{1,0:T(8,128)S(1)}, f32[2048,512]{1,0:T(8,128)}, u32[]{:S(2)}) %copy-start) | copy-done | bytes 4194328
  2.2 1.8 %first_gram.1 = f32[264,256]{1,0:T(8,128)S(1)} custom-call(f32[2048,512]{1,0:T(8,128)S(1)} %copy-done, f32[2048,512]{1,0:T(8,128)S(1)} %copy-done), custom_call_target="tpu_custom_call" | custom-call | tf_op jit(solution)/shard_map/first_gram/pallas_call | solution.py:68
  5.4 6.9 %collective-permute-done = f32[264,256]{1,0:T(8,128)S(1)} collective-permute-done((f32[264,256]{1,0:T(8,128)S(1)}, f32[264,256]{1,0:T(8,128)S(1)}, u32[]{:S(2)}, u32[]{:S(2)}) %collective-permute-start) | collective-permute-done | bytes 270368 | tf_op jit(solution)/shard_map/ppermute | solution.py:317
  12.4 1.6 collective-permute-start.1
  13.9 5.9 %collective-permute-done.1 = f32[264,256]{1,0:T(8,128)S(1)} collective-permute-done((f32[264,256]{1,0:T(8,128)S(1)}, f32[264,256]{1,0:T(8,128)S(1)}, u32[]{:S(2)}, u32[]{:S(2)}) %collective-permute-start.1) | collective-permute-done | bytes 270368 | tf_op jit(solution)/shard_map/ppermute | solution.py:317
  19.9 2.8 %collective-permute-start.2 = (f32[264,256]{1,0:T(8,128)S(1)}, f32[264,256]{1,0:T(8,128)S(1)}, u32[]{:S(2)}, u32[]{:S(2)}) collective-permute-start(f32[264,256]{1,0:T(8,128)S(1)} %add.19.left_ref), channel_id=1, source_target_pairs={{0,6},{1,7},{2,4},{3,5},{4,2},{5,3},{6,0},{7,1},{8,14},{9,15},{10,... | collective-permute-start | bytes 811016 | tf_op jit(solution)/shard_map/ppermute | solution.py:317
  22.7 5.0 %collective-permute-done.2.right_ref = f32[264,256]{1,0:T(8,128)S(1)} collective-permute-done((f32[264,256]{1,0:T(8,128)S(1)}, f32[264,256]{1,0:T(8,128)S(1)}, u32[]{:S(2)}, u32[]{:S(2)}) %collective-permute-start.2) | collective-permute-done | bytes 270368 | tf_op jit(solution)/shard_map/ppermute | solution.py:317
  27.7 14.4 %solve.3 = (bf16[512,512]{1,0:T(8,128)(2,1)S(1)}, bf16[512,512]{1,0:T(8,128)(2,1)S(1)}) custom-call(f32[264,256]{1,0:T(8,128)S(1)} %add.19.left_ref, f32[264,256]{1,0:T(8,128)S(1)} %collective-permute-done.2.right_ref), custom_call_target="tpu_custom_call" | custom-call | tf_op jit(solution)/shard_map/solve/pallas_call | solution.py:162
  44.1 2.0 %collective-permute-start.9 = (f32[1024,256]{1,0:T(8,128)S(1)}, f32[1024,256]{1,0:T(8,128)S(1)}, u32[]{:S(2)}, u32[]{:S(2)}) collective-permute-start(f32[1024,256]{1,0:T(8,128)S(1)} %turn_lower.5), channel_id=1, source_target_pairs={{0,8},{1,9},{2,10},{3,11},{4,12},{5,13},{6,14},{7,15},{8,16},{9,17... | collective-permute-start | bytes 3145736 | tf_op jit(solution)/shard_map/ppermute | solution.py:317
  46.6 1.8 %turn_upper.2.upper_ref.refs_0_ = f32[2048,256]{1,0:T(8,128)S(1)} custom-call(f32[2048,512]{1,0:T(8,128)S(1)} %copy-done.1, bf16[512,512]{1,0:T(8,128)(2,1)S(1)} %get-tuple-element.14.refs_1_, bf16[512,512]{1,0:T(8,128)(2,1)S(1)} %get-tuple-element.15.refs_2_), custom_call_target="tpu_custom_call" | custom-call | tf_op jit(solution)/shard_map/turn_upper/pallas_call | solution.py:204
  48.4 13.5 %collective-permute-done.8.refs_0_ = f32[1024,256]{1,0:T(8,128)S(1)} collective-permute-done((f32[1024,256]{1,0:T(8,128)S(1)}, f32[1024,256]{1,0:T(8,128)S(1)}, u32[]{:S(2)}, u32[]{:S(2)}) %collective-permute-start.8) | collective-permute-done | bytes 1048608 | tf_op jit(solution)/shard_map/ppermute | solution.py:317
  62.0 11.2 %collective-permute-done.9.refs_1_ = f32[1024,256]{1,0:T(8,128)S(1)} collective-permute-done((f32[1024,256]{1,0:T(8,128)S(1)}, f32[1024,256]{1,0:T(8,128)S(1)}, u32[]{:S(2)}, u32[]{:S(2)}) %collective-permute-start.9) | collective-permute-done | bytes 1048608 | tf_op jit(solution)/shard_map/ppermute | solution.py:317
  74.5 3.2 %collective-permute-start.10 = (f32[264,256]{1,0:T(8,128)S(1)}, f32[264,256]{1,0:T(8,128)S(1)}, u32[]{:S(2)}, u32[]{:S(2)}) collective-permute-start(f32[264,256]{1,0:T(8,128)S(1)} %gram.3), channel_id=1, source_target_pairs={{0,1},{1,0},{2,3},{3,2},{4,5},{5,4},{6,7},{7,6},{8,8},{9,9},{10,10... | collective-permute-start | bytes 811016 | tf_op jit(solution)/shard_map/ppermute | solution.py:317
  80.8 2.0 %collective-permute-done.10 = f32[264,256]{1,0:T(8,128)S(1)} collective-permute-done((f32[264,256]{1,0:T(8,128)S(1)}, f32[264,256]{1,0:T(8,128)S(1)}, u32[]{:S(2)}, u32[]{:S(2)}) %collective-permute-start.10) | collective-permute-done | bytes 270368 | tf_op jit(solution)/shard_map/ppermute | solution.py:317
  83.9 5.5 %collective-permute-done.11 = f32[264,256]{1,0:T(8,128)S(1)} collective-permute-done((f32[264,256]{1,0:T(8,128)S(1)}, f32[264,256]{1,0:T(8,128)S(1)}, u32[]{:S(2)}, u32[]{:S(2)}) %collective-permute-start.11) | collective-permute-done | bytes 270368 | tf_op jit(solution)/shard_map/ppermute | solution.py:317
  89.4 2.9 %collective-permute-start.12 = (f32[264,256]{1,0:T(8,128)S(1)}, f32[264,256]{1,0:T(8,128)}, u32[]{:S(2)}, u32[]{:S(2)}) collective-permute-start(f32[264,256]{1,0:T(8,128)S(1)} %add.23.left_ref), channel_id=1, source_target_pairs={{0,6},{1,7},{2,4},{3,5},{4,2},{5,3},{6,0},{7,1},{8,14},{9,15},{10,... | collective-permute-start | bytes 811016 | tf_op jit(solution)/shard_map/ppermute | solution.py:317
  93.0 3.7 %collective-permute-start.7 = (f32[264,256]{1,0:T(8,128)}, f32[264,256]{1,0:T(8,128)}, u32[]{:S(2)}, u32[]{:S(2)}) collective-permute-start(f32[264,256]{1,0:T(8,128)} %add.21.left_ref), channel_id=1, source_target_pairs={{0,0},{1,1},{2,2},{3,3},{4,4},{5,5},{6,6},{7,7},{8,9},{9,8},{10,11... | collective-permute-start | bytes 811016 | tf_op jit(solution)/shard_map/ppermute | solution.py:317
  97.3 15.3 %solve.5 = (bf16[512,512]{1,0:T(8,128)(2,1)S(1)}, bf16[512,512]{1,0:T(8,128)(2,1)S(1)}) custom-call(f32[264,256]{1,0:T(8,128)S(1)} %add.23.left_ref, f32[264,256]{1,0:T(8,128)} %collective-permute-done.12.right_ref), custom_call_target="tpu_custom_call" | custom-call | tf_op jit(solution)/shard_map/solve/pallas_call | solution.py:162
  112.7 16.5 %solve.4 = (bf16[512,512]{1,0:T(8,128)(2,1)S(1)}, bf16[512,512]{1,0:T(8,128)(2,1)S(1)}) custom-call(f32[264,256]{1,0:T(8,128)} %add.21.left_ref, f32[264,256]{1,0:T(8,128)} %collective-permute-done.7.right_ref), custom_call_target="tpu_custom_call" | custom-call | tf_op jit(solution)/shard_map/solve/pallas_call | solution.py:162
  130.4 1.8 %turn_upper.3.done_ref = f32[2048,256]{1,0:T(8,128)S(1)} custom-call(f32[2048,256]{1,0:T(8,128)S(1)} %turn_upper.2.upper_ref.refs_0_, f32[1024,256]{1,0:T(8,128)S(1)} %copy-done.3, f32[1024,256]{1,0:T(8,128)S(1)} %collective-permute-done.4.refs_1_.refs_2_, bf16[512,512]{1,0:T(8,128)(2,1)S(1)} %get-tuple-element.16.refs_3_.refs_2_, ...), custom_call_target="tpu_custom_call" | custom-call | tf_op jit(solution)/shard_map/turn_upper/pallas_call | solution.py:204
  132.3 4.8 %last_turn.1 = (f32[1024,256]{1,0:T(8,128)S(1)}, f32[1024,256]{1,0:T(8,128)S(1)}, f32[2048,512]{1,0:T(8,128)}) custom-call(s32[1]{0:T(128)} %bitcast.flag_ref, f32[2048,256]{1,0:T(8,128)S(1)} %turn_upper.3.done_ref, f32[2048,256]{1,0:T(8,128)S(1)} %turn_upper.2.upper_ref.refs_0_, f32[1024,256]{1,0:T(8,128)S(1)} %copy-done.5, f32[1024,256]{1,0:T(8,128)S(1)} %copy-done.7, ...), custom_call_target="tpu_custom_call" | custom-call | tf_op jit(solution)/shard_map/last_turn/pallas_call | solution.py:249
  141.3 15.3 %collective-permute-done.15.refs_2_ = f32[1024,256]{1,0:T(8,128)S(1)} collective-permute-done((f32[1024,256]{1,0:T(8,128)S(1)}, f32[1024,256]{1,0:T(8,128)S(1)}, u32[]{:S(2)}, u32[]{:S(2)}) %collective-permute-start.15) | collective-permute-done | bytes 1048608 | tf_op jit(solution)/shard_map/ppermute | solution.py:317
  156.5 11.2 %collective-permute-done.16.refs_3_ = f32[1024,256]{1,0:T(8,128)S(1)} collective-permute-done((f32[1024,256]{1,0:T(8,128)S(1)}, f32[1024,256]{1,0:T(8,128)S(1)}, u32[]{:S(2)}, u32[]{:S(2)}) %collective-permute-start.16) | collective-permute-done | bytes 1048608 | tf_op jit(solution)/shard_map/ppermute | solution.py:317
  167.8 1.5 finish.1
  (46 shorter events, 16.2 us)
Async XLA Ops:
  0.0 2.2 %copy-start = (f32[2048,512]{1,0:T(8,128)S(1)}, f32[2048,512]{1,0:T(8,128)}, u32[]{:S(2)}) copy-start(f32[2048,512]{1,0:T(8,128)} %refs_0_.5) | copy-start | bytes 12582916
  2.2 39.9 %copy-start.1 = (f32[2048,512]{1,0:T(8,128)S(1)}, f32[2048,512]{1,0:T(8,128)}, u32[]{:S(2)}) copy-start(f32[2048,512]{1,0:T(8,128)} %refs_0_.5) | copy-start | bytes 12582916
  4.0 8.3 %collective-permute-start = (f32[264,256]{1,0:T(8,128)S(1)}, f32[264,256]{1,0:T(8,128)S(1)}, u32[]{:S(2)}, u32[]{:S(2)}) collective-permute-start(f32[264,256]{1,0:T(8,128)S(1)} %first_gram.1), channel_id=1, source_target_pairs={{0,1},{1,0},{2,3},{3,2},{4,5},{5,4},{6,7},{7,6},{8,9},{9,8},{10,11... | collective-permute-start | bytes 811016 | tf_op jit(solution)/shard_map/ppermute | solution.py:317
  12.4 7.5 %collective-permute-start.1 = (f32[264,256]{1,0:T(8,128)S(1)}, f32[264,256]{1,0:T(8,128)S(1)}, u32[]{:S(2)}, u32[]{:S(2)}) collective-permute-start(f32[264,256]{1,0:T(8,128)S(1)} %add.18), channel_id=1, source_target_pairs={{0,2},{1,3},{2,0},{3,1},{4,6},{5,7},{6,4},{7,5},{8,10},{9,11},{10,... | collective-permute-start | bytes 811016 | tf_op jit(solution)/shard_map/ppermute | solution.py:317
  19.9 7.8 %collective-permute-start.2 = (f32[264,256]{1,0:T(8,128)S(1)}, f32[264,256]{1,0:T(8,128)S(1)}, u32[]{:S(2)}, u32[]{:S(2)}) collective-permute-start(f32[264,256]{1,0:T(8,128)S(1)} %add.19.left_ref), channel_id=1, source_target_pairs={{0,6},{1,7},{2,4},{3,5},{4,2},{5,3},{6,0},{7,1},{8,14},{9,15},{10,... | collective-permute-start | bytes 811016 | tf_op jit(solution)/shard_map/ppermute | solution.py:317
  44.1 17.9 %collective-permute-start.8 = (f32[1024,256]{1,0:T(8,128)S(1)}, f32[1024,256]{1,0:T(8,128)S(1)}, u32[]{:S(2)}, u32[]{:S(2)}) collective-permute-start(f32[1024,256]{1,0:T(8,128)S(1)} %turn_lower.4), channel_id=1, source_target_pairs={{0,8},{1,9},{2,10},{3,11},{4,12},{5,13},{6,14},{7,15},{8,16},{9,17... | collective-permute-start | bytes 3145736 | tf_op jit(solution)/shard_map/ppermute | solution.py:317
  44.1 29.1 %collective-permute-start.9 = (f32[1024,256]{1,0:T(8,128)S(1)}, f32[1024,256]{1,0:T(8,128)S(1)}, u32[]{:S(2)}, u32[]{:S(2)}) collective-permute-start(f32[1024,256]{1,0:T(8,128)S(1)} %turn_lower.5), channel_id=1, source_target_pairs={{0,8},{1,9},{2,10},{3,11},{4,12},{5,13},{6,14},{7,15},{8,16},{9,17... | collective-permute-start | bytes 3145736 | tf_op jit(solution)/shard_map/ppermute | solution.py:317
  46.1 31.5 %collective-permute-start.3 = (f32[1024,256]{1,0:T(8,128)S(1)}, f32[1024,256]{1,0:T(8,128)S(1)}, u32[]{:S(2)}, u32[]{:S(2)}) collective-permute-start(f32[1024,256]{1,0:T(8,128)S(1)} %turn_lower.4), channel_id=1, source_target_pairs={{0,8},{1,9},{2,10},{3,11},{4,12},{5,13},{6,14},{7,15},{8,0},{9,1},... | collective-permute-start | bytes 3145736 | tf_op jit(solution)/shard_map/ppermute | solution.py:317
  46.2 31.4 %collective-permute-start.4 = (f32[1024,256]{1,0:T(8,128)S(1)}, f32[1024,256]{1,0:T(8,128)S(1)}, u32[]{:S(2)}, u32[]{:S(2)}) collective-permute-start(f32[1024,256]{1,0:T(8,128)S(1)} %turn_lower.5), channel_id=1, source_target_pairs={{0,8},{1,9},{2,10},{3,11},{4,12},{5,13},{6,14},{7,15},{8,0},{9,1},... | collective-permute-start | bytes 3145736 | tf_op jit(solution)/shard_map/ppermute | solution.py:317
  62.0 17.0 %copy-start.4 = (f32[1024,256]{1,0:T(8,128)}, f32[1024,256]{1,0:T(8,128)S(1)}, u32[]{:S(2)}) copy-start(f32[1024,256]{1,0:T(8,128)S(1)} %collective-permute-done.8.refs_0_) | copy-start | bytes 3145732
  73.2 5.7 %copy-start.6 = (f32[1024,256]{1,0:T(8,128)}, f32[1024,256]{1,0:T(8,128)S(1)}, u32[]{:S(2)}) copy-start(f32[1024,256]{1,0:T(8,128)S(1)} %collective-permute-done.9.refs_1_) | copy-start | bytes 3145732
  74.5 8.4 %collective-permute-start.10 = (f32[264,256]{1,0:T(8,128)S(1)}, f32[264,256]{1,0:T(8,128)S(1)}, u32[]{:S(2)}, u32[]{:S(2)}) collective-permute-start(f32[264,256]{1,0:T(8,128)S(1)} %gram.3), channel_id=1, source_target_pairs={{0,1},{1,0},{2,3},{3,2},{4,5},{5,4},{6,7},{7,6},{8,8},{9,9},{10,10... | collective-permute-start | bytes 811016 | tf_op jit(solution)/shard_map/ppermute | solution.py:317
  79.9 3.3 %collective-permute-start.5 = (f32[264,256]{1,0:T(8,128)S(1)}, f32[264,256]{1,0:T(8,128)S(1)}, u32[]{:S(2)}, u32[]{:S(2)}) collective-permute-start(f32[264,256]{1,0:T(8,128)S(1)} %gram.2), channel_id=1, source_target_pairs={{0,0},{1,1},{2,2},{3,3},{4,4},{5,5},{6,6},{7,7},{8,10},{9,11},{10,... | collective-permute-start | bytes 811016 | tf_op jit(solution)/shard_map/ppermute | solution.py:317
  82.8 6.5 %collective-permute-start.11 = (f32[264,256]{1,0:T(8,128)S(1)}, f32[264,256]{1,0:T(8,128)S(1)}, u32[]{:S(2)}, u32[]{:S(2)}) collective-permute-start(f32[264,256]{1,0:T(8,128)S(1)} %add.22), channel_id=1, source_target_pairs={{0,2},{1,3},{2,0},{3,1},{4,6},{5,7},{6,4},{7,5},{8,10},{9,11},{10,... | collective-permute-start | bytes 811016 | tf_op jit(solution)/shard_map/ppermute | solution.py:317
  83.3 9.0 %collective-permute-start.6 = (f32[264,256]{1,0:T(8,128)S(1)}, f32[264,256]{1,0:T(8,128)S(1)}, u32[]{:S(2)}, u32[]{:S(2)}) collective-permute-start(f32[264,256]{1,0:T(8,128)S(1)} %add.20), channel_id=1, source_target_pairs={{0,0},{1,1},{2,2},{3,3},{4,4},{5,5},{6,6},{7,7},{8,14},{9,15},{10,... | collective-permute-start | bytes 811016 | tf_op jit(solution)/shard_map/ppermute | solution.py:317
  89.4 7.9 %collective-permute-start.12 = (f32[264,256]{1,0:T(8,128)S(1)}, f32[264,256]{1,0:T(8,128)}, u32[]{:S(2)}, u32[]{:S(2)}) collective-permute-start(f32[264,256]{1,0:T(8,128)S(1)} %add.23.left_ref), channel_id=1, source_target_pairs={{0,6},{1,7},{2,4},{3,5},{4,2},{5,3},{6,0},{7,1},{8,14},{9,15},{10,... | collective-permute-start | bytes 811016 | tf_op jit(solution)/shard_map/ppermute | solution.py:317
  93.0 19.6 %collective-permute-start.7 = (f32[264,256]{1,0:T(8,128)}, f32[264,256]{1,0:T(8,128)}, u32[]{:S(2)}, u32[]{:S(2)}) collective-permute-start(f32[264,256]{1,0:T(8,128)} %add.21.left_ref), channel_id=1, source_target_pairs={{0,0},{1,1},{2,2},{3,3},{4,4},{5,5},{6,6},{7,7},{8,9},{9,8},{10,11... | collective-permute-start | bytes 811016 | tf_op jit(solution)/shard_map/ppermute | solution.py:317
  96.7 35.5 %copy-start.5 = (f32[1024,256]{1,0:T(8,128)S(1)}, f32[1024,256]{1,0:T(8,128)}, u32[]{:S(2)}) copy-start(f32[1024,256]{1,0:T(8,128)} %copy-done.4) | copy-start | bytes 3145732
  129.2 1.2 copy-start.3
  130.4 1.8 %copy-start.7 = (f32[1024,256]{1,0:T(8,128)S(1)}, f32[1024,256]{1,0:T(8,128)}, u32[]{:S(2)}) copy-start(f32[1024,256]{1,0:T(8,128)} %copy-done.6) | copy-start | bytes 3145732
  137.0 2.9 %collective-permute-start.13 = (f32[1024,256]{1,0:T(8,128)S(1)}, f32[1024,256]{1,0:T(8,128)S(1)}, u32[]{:S(2)}, u32[]{:S(2)}) collective-permute-start(f32[1024,256]{1,0:T(8,128)S(1)} %get-tuple-element.21), channel_id=1, source_target_pairs={{0,8},{1,9},{2,10},{3,11},{4,12},{5,13},{6,14},{7,15},{8,0},{9,1},... | collective-permute-start | bytes 3145736 | tf_op jit(solution)/shard_map/ppermute | solution.py:317
  137.1 4.1 %collective-permute-start.14 = (f32[1024,256]{1,0:T(8,128)S(1)}, f32[1024,256]{1,0:T(8,128)S(1)}, u32[]{:S(2)}, u32[]{:S(2)}) collective-permute-start(f32[1024,256]{1,0:T(8,128)S(1)} %get-tuple-element.22), channel_id=1, source_target_pairs={{0,8},{1,9},{2,10},{3,11},{4,12},{5,13},{6,14},{7,15},{8,0},{9,1},... | collective-permute-start | bytes 3145736 | tf_op jit(solution)/shard_map/ppermute | solution.py:317
  138.6 17.9 %collective-permute-start.15 = (f32[1024,256]{1,0:T(8,128)S(1)}, f32[1024,256]{1,0:T(8,128)S(1)}, u32[]{:S(2)}, u32[]{:S(2)}) collective-permute-start(f32[1024,256]{1,0:T(8,128)S(1)} %turn_lower.6), channel_id=1, source_target_pairs={{0,8},{1,9},{2,10},{3,11},{4,12},{5,13},{6,14},{7,15},{8,16},{9,17... | collective-permute-start | bytes 3145736 | tf_op jit(solution)/shard_map/ppermute | solution.py:317
  139.8 28.0 %collective-permute-start.16 = (f32[1024,256]{1,0:T(8,128)S(1)}, f32[1024,256]{1,0:T(8,128)S(1)}, u32[]{:S(2)}, u32[]{:S(2)}) collective-permute-start(f32[1024,256]{1,0:T(8,128)S(1)} %turn_lower.7), channel_id=1, source_target_pairs={{0,8},{1,9},{2,10},{3,11},{4,12},{5,13},{6,14},{7,15},{8,16},{9,17... | collective-permute-start | bytes 3145736 | tf_op jit(solution)/shard_map/ppermute | solution.py:317
  (1 other events, 1.0 us)
